TPU v7x, 32 devices: a whole 2x2x4 slice. The times are simulated.
32 devices in a mesh: segment: 16 (over z, x, core), slab: 2 (over y).
Axes of the slice: x: 2, y: 2, z: 4, core: 2. Of those that a mesh axis runs over, the one named last changes fastest.
Arguments:
- fwd_in: bfloat16 [16, 2, 32, 4, 4, 128], P('segment', None, None, 'slab'), may hold values from -6 to 6
- back_out: bfloat16 [16, 2, 32, 4, 4, 128], P('segment', None, None, 'slab'), may hold values from -6 to 6
- back_grad: bfloat16 [16, 2, 32, 4, 4, 128], P('segment', None, None, 'slab'), may hold values from -6 to 6
- batch_next: bfloat16 [2, 32, 4, 4, 128], P(None, None, 'slab'), may hold values from -6 to 6
- loss_grad: bfloat16 [2, 2, 32, 4, 4, 128], P(None, None, None, 'slab'), may hold values from -6 to 6
- weights: bfloat16 [16, 2, 32, 864], P('segment'), may hold values from -0.21875 to 0.21875
Outputs:
- fwd_out: bfloat16 [16, 2, 32, 4, 4, 128], P('segment', None, None, 'slab')
- back_acts: bfloat16 [16, 2, 32, 4, 4, 128], P('segment', None, None, 'slab')
- back_grads: bfloat16 [16, 2, 32, 4, 4, 128], P('segment', None, None, 'slab')
- weight_grads: float32 [16, 2, 32, 864], P('segment', None, None, 'slab')
All inputs are finite; a program needn't handle non-finite values.
Results may differ from a plain program's by a relative error of at most 0.012.
Values may be sent and summed in bfloat16 or wider, within the bound.
A program may use at most 64 MiB of HBM per device.

v0:
```python
import functools

import jax
import jax.numpy as jnp
from jax import lax
from jax.experimental import pallas as pl
from jax.experimental.pallas import tpu as pltpu
from jax.sharding import PartitionSpec as P

MESH = pl.DeviceIdType.MESH
F, G, FT, GT = range(4)
X1, X2, O1, O2, G1, G2 = range(6)
Y1, Y2, R1, R2, E1, E2 = range(6)
PX, PH, PD, PY, PU, PE = range(6)


def sigmoid(v):
    return 1.0 / (1.0 + jnp.exp(-v))


def silu(v):
    return v / (1.0 + jnp.exp(-v))


def slope(v):
    sig = sigmoid(v)
    return sig * (1.0 + v * (1.0 - sig))


def kernel(
    dims, fwd_hbm, bout_hbm, bgrad_hbm, nxt_hbm, loss_hbm, kern_hbm, fout, backs, grads, dw,
    fwd, bout, bgrad, nxt, loss, kern, kt, w, dt, pad, stage, second, made, nat, acc, g3, dsum, dpart, dgot,
    halo_s, halo_r, seg_s, seg_r, out_s, d_s, d_r, in_s,
):
    C, D, H, W, segs, n, scale = dims
    DH, HW = D * H, H * W
    cs = C // n
    LW = pl.cdiv(3 * C, 128) * 128
    f32, bf16 = jnp.float32, jnp.bfloat16
    seg = lax.axis_index("segment")
    slab = lax.axis_index("slab")
    has_prev, has_next = seg > 0, seg < segs - 1
    is_first, is_last = seg == 0, seg == segs - 1
    prev_seg = lax.rem(seg + segs - 1, segs)
    next_seg = lax.rem(seg + 1, segs)
    lane_no = lax.broadcasted_iota(jnp.int32, (C, W), 1)

    fetches = [
        pltpu.make_async_copy(src, dst, in_s.at[i])
        for i, (src, dst) in enumerate(
            [
                (bgrad_hbm, bgrad), (bout_hbm, bout), (fwd_hbm, fwd),
                (kern_hbm, kern), (nxt_hbm, nxt), (loss_hbm, loss),
            ]
        )
    ]
    for fetch in fetches:
        fetch.start()

    barrier = pltpu.get_barrier_semaphore()

    @pl.when(has_prev)
    def _():
        pl.semaphore_signal(barrier, inc=1, device_id={"segment": prev_seg}, device_id_type=MESH)

    @pl.when(has_next)
    def _():
        pl.semaphore_signal(barrier, inc=1, device_id={"segment": next_seg}, device_id_type=MESH)

    for k in range(1, n):
        pl.semaphore_signal(
            barrier, inc=1, device_id={"slab": lax.rem(slab + k, n)}, device_id_type=MESH
        )

    def lane(q, hh):
        return (q * (H + 2) + hh) * W

    zero = jnp.zeros((C, W), bf16)
    for t in range(2):
        for k in range(6):
            for q in range(D + 2):
                for hh in (0, H + 1):
                    pad[t, k, :, pl.ds(lane(q, hh), W)] = zero

    @pl.when(slab == 0)
    def _():
        for t in range(2):
            for k in range(6):
                pad[t, k, :, pl.ds(lane(0, 1), HW)] = jnp.zeros((C, HW), bf16)

    @pl.when(slab == n - 1)
    def _():
        for t in range(2):
            for k in range(6):
                pad[t, k, :, pl.ds(lane(D + 1, 1), HW)] = jnp.zeros((C, HW), bf16)

    def load_stage(slot, ref, s):
        stage[slot] = ref[s].astype(f32)

    def staged(slot, r):
        return stage[slot, pl.ds(r, C, stride=DH), :]

    def prepare_weights():
        fetches[3].wait()
        wide = kern[...].astype(f32)
        kt[...] = jnp.concatenate([wide, jnp.zeros((LW - 2 * C, 27 * C), f32)], axis=0).T

        def tap(t):
            return kt[pl.ds(t, C, stride=27), :]

        for a in range(3):
            for c in range(3):
                block = jnp.concatenate([tap(9 * a + 3 * b + c) for b in range(3)], axis=0).T
                for f in range(2):
                    w[F + f, a, c * C : (c + 1) * C, :] = block[f * C : (f + 1) * C].astype(bf16)
                for f in range(2):
                    turned = jnp.concatenate(
                        [
                            tap(9 * (2 - a) + 3 * (2 - b) + 2 - c)[:, f * C : (f + 1) * C]
                            for b in range(3)
                        ],
                        axis=1,
                    )
                    w[FT + f, a, c * C : (c + 1) * C, :] = turned.astype(bf16)

    def load_pair(i, slot, ref):
        fetches[i].wait()
        for s in range(2):
            load_stage(slot + s, ref, s)

    def halo(t, k, up):
        src_q, dst_q = (D, 0) if up else (1, D + 1)
        target = lax.rem(slab + (1 if up else n - 1), n)
        return pltpu.make_async_remote_copy(
            src_ref=pad.at[t, k, :, pl.ds(lane(src_q, 1), HW)],
            dst_ref=pad.at[t, k, :, pl.ds(lane(dst_q, 1), HW)],
            send_sem=halo_s.at[t, k, up],
            recv_sem=halo_r.at[t, k, up],
            device_id={"slab": target},
            device_id_type=MESH,
        )

    def halo_start(t, k):
        @pl.when(slab < n - 1)
        def _():
            halo(t, k, 1).start()

        @pl.when(slab > 0)
        def _():
            halo(t, k, 0).start()

    def halo_arrived(t, k):
        @pl.when(slab > 0)
        def _():
            halo(t, k, 1).wait_recv()

        @pl.when(slab < n - 1)
        def _():
            halo(t, k, 0).wait_recv()

    def halo_sent(t, k):
        @pl.when(slab < n - 1)
        def _():
            halo(t, k, 1).wait_send()

        @pl.when(slab > 0)
        def _():
            halo(t, k, 0).wait_send()

    def to_next(k):
        return pltpu.make_async_remote_copy(
            src_ref=made.at[0, k], dst_ref=second.at[X1 + k],
            send_sem=seg_s.at[0, k], recv_sem=seg_r.at[0, k],
            device_id={"segment": next_seg}, device_id_type=MESH,
        )

    def to_prev(k):
        return pltpu.make_async_remote_copy(
            src_ref=made.at[0, k], dst_ref=second.at[k],
            send_sem=seg_s.at[0, k], recv_sem=seg_r.at[0, k],
            device_id={"segment": prev_seg}, device_id_type=MESH,
        )

    def out_prev(k):
        dst = backs.at[k - R1] if k < E1 else grads.at[k - E1]
        return pltpu.make_async_remote_copy(
            src_ref=nat.at[k], dst_ref=dst,
            send_sem=seg_s.at[1, k], recv_sem=seg_r.at[1, k],
            device_id={"segment": prev_seg}, device_id_type=MESH,
        )

    def own_out(k):
        return pltpu.make_async_copy(nat.at[k], fout.at[k], out_s.at[k])

    def last_act(k):
        return pltpu.make_async_copy(nat.at[k], backs.at[k], out_s.at[2 + k])

    def last_grad(k):
        return pltpu.make_async_copy(loss.at[2 + k], grads.at[k], out_s.at[4 + k])

    def put(t, k, r, value):
        d, h = divmod(r, H)
        pad[t, k, :, pl.ds(lane(d + 1, h + 1), W)] = value.astype(bf16)

    def tall(t, k, q):
        return jnp.concatenate([pad[t, k, :, pl.ds(lane(q, b), HW)] for b in range(3)], axis=0)

    def conv_local(t, k, m, slot):
        for p in range(D):
            total = None
            for a in range(3):
                if 1 <= p + a <= D:
                    part = jnp.dot(w[m, a], tall(t, k, p + a), preferred_element_type=f32)
                    total = part if total is None else total + part
            acc[slot, :, pl.ds(p * HW, HW)] = total

    def conv_finish(t, k, m, slot):
        for p in range(D):
            total = acc[slot, :, pl.ds(p * HW, HW)]
            for a in range(3):
                if not 1 <= p + a <= D:
                    total += jnp.dot(w[m, a], tall(t, k, p + a), preferred_element_type=f32)
            for h in range(H):
                y = total[:, h * W : (h + 1) * W]
                left = jnp.where(lane_no == 0, 0.0, pltpu.roll(y[:C], 1, 1))
                right = jnp.where(lane_no == W - 1, 0.0, pltpu.roll(y[2 * C :], W - 1, 1))
                yield p * H + h, y[C : 2 * C] + left + right

    def widen(j, r, v):
        at = pl.ds(r * W, W)
        g3[j, 0:C, at] = jnp.where(lane_no == W - 1, 0.0, pltpu.roll(v, W - 1, 1)).astype(bf16)
        g3[j, C : 2 * C, at] = v.astype(bf16)
        g3[j, 2 * C : 3 * C, at] = jnp.where(lane_no == 0, 0.0, pltpu.roll(v, 1, 1)).astype(bf16)

    def wgrad(t, k, j):
        total = None
        for p in range(D):
            lhs = jnp.concatenate([tall(t, k, p + a) for a in range(3)], axis=0)
            part = lax.dot_general(
                lhs, g3[j, :, pl.ds(p * HW, HW)], (((1,), (1,)), ((), ())),
                preferred_element_type=f32,
            )
            total = part if total is None else total + part
        if t == 0:
            dsum[j] = total
            return
        total += dsum[j]
        total = jnp.concatenate([total, jnp.zeros((9 * C, LW - 3 * C), f32)], axis=1)
        for q in range(n):
            for ab in range(9):
                dpart[j, q, ab] = total[ab * C + q * cs : ab * C + (q + 1) * cs]
        for q in range(1, n):
            share(j, q).start()

    def share(j, q):
        target = lax.rem(slab + q, n)
        return pltpu.make_async_remote_copy(
            src_ref=dpart.at[j, target], dst_ref=dgot.at[j, q],
            send_sem=d_s.at[j, q], recv_sem=d_r.at[j, q],
            device_id={"slab": target}, device_id_type=MESH,
        )

    def keep(t, k, r, value):
        held = value.astype(bf16)
        made[t, k, :, pl.ds(r * W, W)] = held
        wide = held.astype(f32)
        if t == 1:
            stage[k, pl.ds(r, C, stride=DH), :] = wide
        return wide

    def send_made(t, k):
        if t == 0:
            if k < R1:
                @pl.when(has_next)
                def _():
                    to_next(k).start()

                @pl.when(is_last)
                def _():
                    second[O1 + k] = made[0, k]
            else:
                @pl.when(has_prev)
                def _():
                    to_prev(k).start()
            return
        nat[k] = stage[k].astype(bf16)
        if k < R1:
            own_out(k).start()

            @pl.when(is_last)
            def _():
                last_act(k).start()
        else:
            @pl.when(has_prev)
            def _():
                out_prev(k).start()

    def tick(t, get, ready):
        if t == 0:
            load_pair(0, G1, bgrad)
        ready(G2)
        for r in range(DH):
            put(t, PD, r, get(G2, r))
        if t == 0:
            peers = has_prev.astype(jnp.int32) + has_next.astype(jnp.int32) + n - 1
            pl.semaphore_wait(barrier, peers)
        halo_start(t, PD)
        if t == 0:
            load_pair(1, O1, bout)
        ready(O1)
        for r in range(DH):
            put(t, PH, r, silu(get(O1, r)))
        halo_start(t, PH)
        if t == 0:
            load_pair(2, X1, fwd)
        ready(X2)
        for r in range(DH):
            put(t, PX, r, silu(get(X2, r)))
        halo_start(t, PX)
        if t == 0:
            prepare_weights()
        conv_local(t, PD, GT, 0)
        conv_local(t, PH, G, 1)
        conv_local(t, PX, F, 2)
        for r in range(DH):
            widen(1, r, get(G2, r))

        ready(G1)
        halo_arrived(t, PD)
        for r, out in conv_finish(t, PD, GT, 0):
            put(t, PE, r, keep(t, E1, r, get(G1, r) + slope(get(O1, r)) * out))
        halo_start(t, PE)
        send_made(t, E1)
        ready(O2)
        halo_arrived(t, PH)
        for r, out in conv_finish(t, PH, G, 1):
            put(t, PU, r, silu(keep(t, R2, r, get(O2, r) - out)))
        halo_start(t, PU)
        send_made(t, R2)
        ready(X1)
        halo_arrived(t, PX)
        for r, out in conv_finish(t, PX, F, 2):
            put(t, PY, r, silu(keep(t, Y1, r, get(X1, r) + out)))
        halo_start(t, PY)
        send_made(t, Y1)

        conv_local(t, PE, FT, 0)
        conv_local(t, PU, F, 1)
        conv_local(t, PY, G, 2)
        wgrad(t, PH, 1)
        for r in range(DH):
            widen(0, r, made[t, E1, :, pl.ds(r * W, W)].astype(f32))

        halo_arrived(t, PE)
        for r, out in conv_finish(t, PE, FT, 0):
            v = made[t, R2, :, pl.ds(r * W, W)].astype(f32)
            keep(t, E2, r, get(G2, r) + slope(v) * out)
        send_made(t, E2)
        halo_arrived(t, PU)
        if t == 1:
            wgrad(t, PU, 0)
        for r, out in conv_finish(t, PU, F, 1):
            keep(t, R1, r, get(O1, r) - out)
        send_made(t, R1)
        halo_arrived(t, PY)
        for r, out in conv_finish(t, PY, G, 2):
            keep(t, Y2, r, get(X2, r) + out)
        send_made(t, Y2)
        if t == 0:
            wgrad(t, PU, 0)

    tick(0, staged, lambda k: None)

    fetches[4].wait()
    fetches[5].wait()

    @pl.when(is_first)
    def _():
        for s in range(2):
            load_stage(X1 + s, nxt, s)
            for r in range(DH):
                second[X1 + s, :, pl.ds(r * W, W)] = staged(X1 + s, r).astype(bf16)

    @pl.when(is_last)
    def _():
        for s in range(2):
            last_grad(s).start()
            load_stage(G1 + s, loss, s)
            for r in range(DH):
                second[G1 + s, :, pl.ds(r * W, W)] = staged(G1 + s, r).astype(bf16)

    def arrived(k):
        if k <= X2:
            @pl.when(has_prev)
            def _():
                to_next(k).wait_recv()
        else:
            @pl.when(has_next)
            def _():
                to_prev(k).wait_recv()

    tick(1, lambda k, r: second[k, :, pl.ds(r * W, W)].astype(f32), arrived)

    for j in (1, 0):
        for q in range(1, n):
            share(j, q).wait_recv()
        total = dpart[j, slab]
        for q in range(1, n):
            total += dgot[j, q]
        total *= scale
        for ab in range(9):
            for c in range(3):
                tap = total[ab] if c == 0 else pltpu.roll(total[ab], LW - c * C, 1)
                dt[j, pl.ds(3 * ab + c, cs, stride=27), :] = tap
        dw[j] = dt[j].T[:C]

    for t in range(2):
        for k in range(6):
            halo_sent(t, k)
    for j in range(2):
        for q in range(1, n):
            share(j, q).wait_send()
    for k in (Y1, Y2):
        own_out(k).wait()

    @pl.when(is_last)
    def _():
        for k in (Y1, Y2):
            last_act(k).wait()
            last_grad(k).wait()

    @pl.when(has_next)
    def _():
        for k in (Y1, Y2):
            to_next(k).wait_send()
        for k in (R1, R2, E1, E2):
            out_prev(k).wait_recv()

    @pl.when(has_prev)
    def _():
        for k in (R1, R2, E1, E2):
            to_prev(k).wait_send()
            out_prev(k).wait_send()


def write_out(*refs):
    srcs, dsts, tiles, sems = refs[:4], refs[4:8], refs[8:12], refs[12]
    reads = [pltpu.make_async_copy(a, b, sems.at[0, i]) for i, (a, b) in enumerate(zip(srcs, tiles))]
    writes = [pltpu.make_async_copy(a, b, sems.at[1, i]) for i, (a, b) in enumerate(zip(tiles, dsts))]
    for read in reads:
        read.start()
    for read, write in zip(reads, writes):
        read.wait()
        write.start()
    for write in writes:
        write.wait()


def local(segs, n, fwd_in, back_out, back_grad, batch_next, loss_grad, weights):
    _, _, C, D, H, W = fwd_in.shape
    rows = C * D * H
    cs = C // n
    f32, bf16 = jnp.float32, jnp.bfloat16
    scale = float(D * n * H * W) ** (-0.5)
    vmem = pl.BlockSpec(memory_space=pltpu.VMEM)
    hbm = pl.BlockSpec(memory_space=pltpu.HBM)
    wide = pl.cdiv(3 * C, 128) * 128
    anywhere = pl.BlockSpec(memory_space=pl.ANY)
    pair = jax.ShapeDtypeStruct((2, rows, W), bf16)
    share = jax.ShapeDtypeStruct((2, C, 27 * cs), f32)
    dma = pltpu.SemaphoreType.DMA
    fout, backs, grads, dw = pl.pallas_call(
        functools.partial(kernel, (C, D, H, W, segs, n, scale)),
        out_shape=(pair, pair, pair, share),
        in_specs=[hbm] * 6,
        out_specs=(anywhere, anywhere, anywhere, vmem),
        scratch_shapes=[
            pltpu.VMEM((2, rows, W), bf16),
            pltpu.VMEM((2, rows, W), bf16),
            pltpu.VMEM((2, rows, W), bf16),
            pltpu.VMEM((2, rows, W), bf16),
            pltpu.VMEM((4, rows, W), bf16),
            pltpu.VMEM((2 * C, 27 * C), bf16),
            pltpu.VMEM((27 * C, wide), f32),
            pltpu.VMEM((4, 3, 3 * C, 3 * C), bf16),
            pltpu.VMEM((2, 27 * cs, wide), f32),
            pltpu.VMEM((2, 6, C, (D + 2) * (H + 2) * W), bf16),
            pltpu.VMEM((6, rows, W), f32),
            pltpu.VMEM((6, C, D * H * W), bf16),
            pltpu.VMEM((2, 6, C, D * H * W), bf16),
            pltpu.VMEM((6, rows, W), bf16),
            pltpu.VMEM((3, 3 * C, D * H * W), f32),
            pltpu.VMEM((2, 3 * C, D * H * W), bf16),
            pltpu.VMEM((2, 9 * C, 3 * C), f32),
            pltpu.VMEM((2, n, 9, cs, wide), f32),
            pltpu.VMEM((2, n, 9, cs, wide), f32),
            dma((2, 6, 2)),
            dma((2, 6, 2)),
            dma((2, 6)),
            dma((2, 6)),
            dma((6,)),
            dma((2, n)),
            dma((2, n)),
            dma((6,)),
        ],
        compiler_params=pltpu.CompilerParams(
            collective_id=0, has_side_effects=True, vmem_limit_bytes=67043328
        ),
        name="petra",
    )(
        fwd_in.reshape(2, rows, W),
        back_out.reshape(2, rows, W),
        back_grad.reshape(2, rows, W),
        batch_next.reshape(2, rows, W),
        loss_grad.reshape(4, rows, W),
        weights.reshape(2 * C, 27 * C),
    )
    fout, backs, grads, dw = pl.pallas_call(
        write_out,
        out_shape=(pair, pair, pair, share),
        in_specs=[hbm] * 4,
        out_specs=(hbm,) * 4,
        scratch_shapes=[pltpu.VMEM(x.shape, x.dtype) for x in (pair, pair, pair, share)]
        + [dma((2, 4))],
        compiler_params=pltpu.CompilerParams(vmem_limit_bytes=67043328),
        name="write_out",
    )(fout, backs, grads, dw)
    shape = fwd_in.shape
    return fout.reshape(shape), backs.reshape(shape), grads.reshape(shape), dw[None]


def solution(mesh):
    field = P("segment", None, None, "slab", None, None)
    return jax.shard_map(
        functools.partial(local, mesh.shape["segment"], mesh.shape["slab"]),
        mesh=mesh,
        in_specs=(
            field,
            field,
            field,
            P(None, None, "slab", None, None),
            P(None, None, None, "slab", None, None),
            P("segment", None, None, None),
        ),
        out_specs=(field, field, field, P("segment", None, None, "slab")),
        check_vma=False,
    )
```

profile of v0, /device:TPU:1, one launch (start us, length us, event | category | flops | bytes accessed | tf_op | source)
XLA Modules:
  0.0 26.4 jit_solution(4439028943779074650)
XLA Ops:
  0.6 23.9 %petra.1 = (bf16[2,256,128]{2,1,0:T(8,128)(2,1)}, bf16[2,256,128]{2,1,0:T(8,128)(2,1)}, bf16[2,256,128]{2,1,0:T(8,128)(2,1)}, f32[2,32,432]{2,1,0:T(8,128)}) custom-call(bf16[2,256,128]{2,1,0:T(8,128)(2,1)} %bitcast.11, bf16[2,256,128]{2,1,0:T(8,128)(2,1)} %bitcast.12, bf16[2,256,128]{2,1,0:T(8,128)(2,1)} %bitcast.13, bf16[2,256,128]{2,1,0:T(8,128)(2,1)} %bitcast.14, ...), custom_call_target="tpu_custom_call" | custom-call | tf_op jit(solution)/shard_map/petra/pallas_call | solution.py:472
  24.6 1.8 %write_out.1 = (bf16[2,256,128]{2,1,0:T(8,128)(2,1)}, bf16[2,256,128]{2,1,0:T(8,128)(2,1)}, bf16[2,256,128]{2,1,0:T(8,128)(2,1)}, f32[2,32,432]{2,1,0:T(8,128)}) custom-call(bf16[2,256,128]{2,1,0:T(8,128)(2,1)} %get-tuple-element.12.refs_0_, bf16[2,256,128]{2,1,0:T(8,128)(2,1)} %get-tuple-element.13.refs_1_, bf16[2,256,128]{2,1,0:T(8,128)(2,1)} %get-tuple-element.14.refs_2_, ...), custom_call_target="tpu_custom_call" | custom-call | tf_op jit(solution)/shard_map/write_out/pallas_call | solution.py:518
where the time goes:
time: 26.8 us; the launch traced here: 26.4 us
  Pallas kernels  25.8 us (96%)
  between operations  0.64 us (2%)
    pallas_call x1, Pallas kernels, local(): pl.pallas_call(functools.partial(kernel, (C, D, H, W, segs, n, scale)), o...  23.9 us
    pallas_call x1, Pallas kernels, local(): pl.pallas_call(write_out, out_shape=(pair, pair, pair, share), in_specs=[...  1.82 us

commit v1 on v0

--- a/solution.py
+++ b/solution.py
@@ -444,13 +444,9 @@
 
 
 def write_out(*refs):
-    srcs, dsts, tiles, sems = refs[:4], refs[4:8], refs[8:12], refs[12]
-    reads = [pltpu.make_async_copy(a, b, sems.at[0, i]) for i, (a, b) in enumerate(zip(srcs, tiles))]
-    writes = [pltpu.make_async_copy(a, b, sems.at[1, i]) for i, (a, b) in enumerate(zip(tiles, dsts))]
-    for read in reads:
-        read.start()
-    for read, write in zip(reads, writes):
-        read.wait()
+    srcs, dsts, sems = refs[:4], refs[4:8], refs[8]
+    writes = [pltpu.make_async_copy(a, b, sems.at[i]) for i, (a, b) in enumerate(zip(srcs, dsts))]
+    for write in writes:
         write.start()
     for write in writes:
         write.wait()
@@ -471,9 +467,9 @@
     dma = pltpu.SemaphoreType.DMA
     fout, backs, grads, dw = pl.pallas_call(
         functools.partial(kernel, (C, D, H, W, segs, n, scale)),
-        out_shape=(pair, pair, pair, share),
+        out_shape=tuple(pltpu.VMEM(x.shape, x.dtype) for x in (pair, pair, pair, share)),
         in_specs=[hbm] * 6,
-        out_specs=(anywhere, anywhere, anywhere, vmem),
+        out_specs=(vmem, vmem, vmem, vmem),
         scratch_shapes=[
             pltpu.VMEM((2, rows, W), bf16),
             pltpu.VMEM((2, rows, W), bf16),
@@ -504,25 +500,29 @@
             dma((6,)),
         ],
         compiler_params=pltpu.CompilerParams(
-            collective_id=0, has_side_effects=True, vmem_limit_bytes=67043328
+            collective_id=0, has_side_effects=True, vmem_limit_bytes=48 << 20
         ),
         name="petra",
     )(
-        fwd_in.reshape(2, rows, W),
-        back_out.reshape(2, rows, W),
-        back_grad.reshape(2, rows, W),
-        batch_next.reshape(2, rows, W),
-        loss_grad.reshape(4, rows, W),
-        weights.reshape(2 * C, 27 * C),
+        *[
+            pltpu.with_memory_space_constraint(x, pltpu.HBM)
+            for x in (
+                fwd_in.reshape(2, rows, W),
+                back_out.reshape(2, rows, W),
+                back_grad.reshape(2, rows, W),
+                batch_next.reshape(2, rows, W),
+                loss_grad.reshape(4, rows, W),
+                weights.reshape(2 * C, 27 * C),
+            )
+        ]
     )
     fout, backs, grads, dw = pl.pallas_call(
         write_out,
         out_shape=(pair, pair, pair, share),
-        in_specs=[hbm] * 4,
+        in_specs=[vmem] * 4,
         out_specs=(hbm,) * 4,
-        scratch_shapes=[pltpu.VMEM(x.shape, x.dtype) for x in (pair, pair, pair, share)]
-        + [dma((2, 4))],
-        compiler_params=pltpu.CompilerParams(vmem_limit_bytes=67043328),
+        scratch_shapes=[dma((4,))],
+        compiler_params=pltpu.CompilerParams(vmem_limit_bytes=4 << 20),
         name="write_out",
     )(fout, backs, grads, dw)
     shape = fwd_in.shape

time: 26.8 us -> 25.2 us (0.940)
  Pallas kernels: 25.8 us -> 24.1 us
    pallas_call x1, Pallas kernels: 1.82 us -> 0.82 us  [local(): pl.pallas_call(write_out, out_shape=(pair, pair, pair, share), in_specs=[...]
    pallas_call x1, Pallas kernels: 23.9 us -> 23.3 us  [local(): pl.pallas_call(functools.partial(kernel, (C, D, H, W, segs, n, scale)), o...]
where the time goes in v1:
time: 25.2 us; the launch traced here: 24.8 us
  Pallas kernels  24.1 us (96%)
  between operations  0.64 us (3%)
    pallas_call x1, Pallas kernels, local(): pl.pallas_call(functools.partial(kernel, (C, D, H, W, segs, n, scale)), o...  23.3 us
    pallas_call x1, Pallas kernels, local(): pl.pallas_call(write_out, out_shape=(pair, pair, pair, share), in_specs=[...  0.82 us

profile of v1, /device:TPU:1, one launch (start us, length us, event | category | flops | bytes accessed | tf_op | source)
XLA Modules:
  0.0 24.8 jit_solution(14596657519556956198)
XLA Ops:
  0.6 23.3 %petra.1 = (bf16[2,256,128]{2,1,0:T(8,128)(2,1)S(1)}, bf16[2,256,128]{2,1,0:T(8,128)(2,1)S(1)}, bf16[2,256,128]{2,1,0:T(8,128)(2,1)S(1)}, f32[2,32,432]{2,1,0:T(8,128)S(1)}) custom-call(bf16[2,256,128]{2,1,0:T(8,128)(2,1)} %bitcast.11, bf16[2,256,128]{2,1,0:T(8,128)(2,1)} %bitcast.12, bf16[2,256,128]{2,1,0:T(8,128)(2,1)} %bitcast.13, ...), custom_call_target="tpu_custom_call" | custom-call | tf_op jit(solution)/shard_map/petra/pallas_call | solution.py:468
  23.9 0.8 %write_out.1 = (bf16[2,256,128]{2,1,0:T(8,128)(2,1)}, bf16[2,256,128]{2,1,0:T(8,128)(2,1)}, bf16[2,256,128]{2,1,0:T(8,128)(2,1)}, f32[2,32,432]{2,1,0:T(8,128)}) custom-call(bf16[2,256,128]{2,1,0:T(8,128)(2,1)S(1)} %get-tuple-element.12.refs_0_, bf16[2,256,128]{2,1,0:T(8,128)(2,1)S(1)} %get-tuple-element.13.refs_1_, ...), custom_call_target="tpu_custom_call" | custom-call | tf_op jit(solution)/shard_map/write_out/pallas_call | solution.py:519

commit v2 on v1

v2 whole, which is shorter than its diff:
```python
import functools

import jax
import jax.numpy as jnp
from jax import lax
from jax.experimental import pallas as pl
from jax.experimental.pallas import tpu as pltpu
from jax.sharding import PartitionSpec as P

MESH = pl.DeviceIdType.MESH
F, G, FT, GT = range(4)
X1, X2, O1, O2, G1, G2 = range(6)
Y1, Y2, R1, R2, E1, E2 = range(6)
PX, PH, PD, PY, PU, PE = range(6)


def sigmoid(v):
    return 1.0 / (1.0 + jnp.exp(-v))


def silu(v):
    return v / (1.0 + jnp.exp(-v))


def slope(v):
    sig = sigmoid(v)
    return sig * (1.0 + v * (1.0 - sig))


def kernel(
    dims, fwd_hbm, bout_hbm, bgrad_hbm, nxt_hbm, loss_hbm, kern_hbm, fout, backs, grads, dw,
    fwd, bout, bgrad, nxt, loss, kern, kt, w, dt, pad, stage, second, edge, made, nat, acc, g3,
    dsum, dpart, dgot, halo_s, halo_r, seg_s, seg_r, edge_s, edge_r, out_s, d_s, d_r, in_s, ready_s,
):
    C, D, H, W, segs, n, scale = dims
    DH, HW = D * H, H * W
    cs = C // n
    LW = pl.cdiv(3 * C, 128) * 128
    f32, bf16 = jnp.float32, jnp.bfloat16
    seg = lax.axis_index("segment")
    slab = lax.axis_index("slab")
    has_prev, has_next = seg > 0, seg < segs - 1
    is_first, is_last = seg == 0, seg == segs - 1
    has_below, has_above = slab > 0, slab < n - 1
    prev_seg = lax.rem(seg + segs - 1, segs)
    next_seg = lax.rem(seg + 1, segs)
    below, above = lax.rem(slab + n - 1, n), lax.rem(slab + 1, n)
    lane_no = lax.broadcasted_iota(jnp.int32, (C, W), 1)

    barrier = pltpu.get_barrier_semaphore()

    for k in range(1, n):
        pl.semaphore_signal(
            barrier, inc=1, device_id={"slab": lax.rem(slab + k, n)}, device_id_type=MESH
        )

    @pl.when(has_prev)
    def _():
        pl.semaphore_signal(barrier, inc=1, device_id={"segment": prev_seg}, device_id_type=MESH)

    @pl.when(has_next)
    def _():
        pl.semaphore_signal(barrier, inc=1, device_id={"segment": next_seg}, device_id_type=MESH)

    fetches = [
        pltpu.make_async_copy(src, dst, in_s.at[i])
        for i, (src, dst) in enumerate(
            [
                (bgrad_hbm, bgrad), (bout_hbm, bout), (fwd_hbm, fwd),
                (kern_hbm, kern), (nxt_hbm, nxt), (loss_hbm, loss),
            ]
        )
    ]
    for fetch in fetches:
        fetch.start()

    def lane(q, hh):
        return ((q + 2) * (H + 2) + hh) * W

    zero = jnp.zeros((C, W), bf16)
    for t in range(2):
        for k in range(6):
            reach = 2 if t == 1 and k in (PH, PD) else 1
            for q in range(-reach, D + reach):
                for hh in (0, H + 1):
                    pad[t, k, :, pl.ds(lane(q, hh), W)] = zero

    @pl.when(slab == 0)
    def _():
        for t in range(2):
            for k in range(6):
                pad[t, k, :, pl.ds(lane(-1, 1), HW)] = jnp.zeros((C, HW), bf16)

    @pl.when(slab == n - 1)
    def _():
        for t in range(2):
            for k in range(6):
                pad[t, k, :, pl.ds(lane(D, 1), HW)] = jnp.zeros((C, HW), bf16)

    def load_stage(slot, ref, s):
        stage[slot] = ref[s].astype(f32)

    def staged(slot, r):
        return stage[slot, pl.ds(r, C, stride=DH), :]

    def prepare_weights():
        fetches[3].wait()
        wide = kern[...].astype(f32)
        kt[...] = jnp.concatenate([wide, jnp.zeros((LW - 2 * C, 27 * C), f32)], axis=0).T

        def tap(t):
            return kt[pl.ds(t, C, stride=27), :]

        for a in range(3):
            for c in range(3):
                block = jnp.concatenate([tap(9 * a + 3 * b + c) for b in range(3)], axis=0).T
                for f in range(2):
                    w[F + f, a, c * C : (c + 1) * C, :] = block[f * C : (f + 1) * C].astype(bf16)
                for f in range(2):
                    turned = jnp.concatenate(
                        [
                            tap(9 * (2 - a) + 3 * (2 - b) + 2 - c)[:, f * C : (f + 1) * C]
                            for b in range(3)
                        ],
                        axis=1,
                    )
                    w[FT + f, a, c * C : (c + 1) * C, :] = turned.astype(bf16)

    def load_pair(i, slot, ref):
        fetches[i].wait()
        for s in range(2):
            load_stage(slot + s, ref, s)

    def halo(t, k, side):
        src_q, dst_q = (D - 1, -1) if side == 0 else (0, D)
        return pltpu.make_async_remote_copy(
            src_ref=pad.at[t, k, :, pl.ds(lane(src_q, 1), HW)],
            dst_ref=pad.at[t, k, :, pl.ds(lane(dst_q, 1), HW)],
            send_sem=halo_s.at[t, k, side],
            recv_sem=halo_r.at[t, k, side],
            device_id={"slab": above if side == 0 else below},
            device_id_type=MESH,
        )

    def by_side(to):
        return ((0, has_above), (1, has_below)) if to else ((0, has_below), (1, has_above))

    def halo_start(t, k):
        for side, there in by_side(True):
            @pl.when(there)
            def _():
                halo(t, k, side).start()

    def halo_arrived(t, k):
        for side, there in by_side(False):
            @pl.when(there)
            def _():
                halo(t, k, side).wait_recv()

    def halo_sent(t, k):
        for side, there in by_side(True):
            @pl.when(there)
            def _():
                halo(t, k, side).wait_send()

    def to_seg(k):
        return pltpu.make_async_remote_copy(
            src_ref=made.at[0, k], dst_ref=second.at[k],
            send_sem=seg_s.at[0, k], recv_sem=seg_r.at[0, k],
            device_id={"segment": next_seg if k <= X2 else prev_seg}, device_id_type=MESH,
        )

    def edge_planes(k):
        return 2 if k in (O1, G2) else 1

    def edge_copy(src, k, side, target, which):
        planes = edge_planes(k)
        src_at, dst_at = ((D - planes) * HW, (2 - planes) * HW) if side == 0 else (0, 0)
        return pltpu.make_async_remote_copy(
            src_ref=src.at[:, pl.ds(src_at, planes * HW)],
            dst_ref=edge.at[k, side, :, pl.ds(dst_at, planes * HW)],
            send_sem=edge_s.at[which, k, side], recv_sem=edge_r.at[k, side],
            device_id={"segment": target, "slab": above if side == 0 else below},
            device_id_type=MESH,
        )

    def edge_start(src, k, target, which):
        for side, there in by_side(True):
            @pl.when(there)
            def _():
                edge_copy(src, k, side, target, which).start()

    def edge_sent(src, k, target, which):
        for side, there in by_side(True):
            @pl.when(there)
            def _():
                edge_copy(src, k, side, target, which).wait_send()

    def out_prev(k):
        dst = backs.at[k - R1] if k < E1 else grads.at[k - E1]
        return pltpu.make_async_remote_copy(
            src_ref=nat.at[k], dst_ref=dst,
            send_sem=seg_s.at[1, k], recv_sem=seg_r.at[1, k],
            device_id={"segment": prev_seg}, device_id_type=MESH,
        )

    def own_out(k):
        return pltpu.make_async_copy(nat.at[k], fout.at[k], out_s.at[k])

    def last_act(k):
        return pltpu.make_async_copy(nat.at[k], backs.at[k], out_s.at[2 + k])

    def last_grad(k):
        return pltpu.make_async_copy(loss.at[2 + k], grads.at[k], out_s.at[4 + k])

    def put(t, k, r, value):
        d, h = divmod(r, H)
        pad[t, k, :, pl.ds(lane(d, h + 1), W)] = value.astype(bf16)

    def tall(t, k, q):
        return jnp.concatenate([pad[t, k, :, pl.ds(lane(q, b), HW)] for b in range(3)], axis=0)

    def taps(t, k, m, p, which):
        total = None
        for a in which:
            part = jnp.dot(w[m, a], tall(t, k, p + a - 1), preferred_element_type=f32)
            total = part if total is None else total + part
        return total

    def inner(p):
        return [a for a in range(3) if 0 <= p + a - 1 < D]

    def outer(p):
        return [a for a in range(3) if not 0 <= p + a - 1 < D]

    def conv_local(t, k, m, slot):
        for p in range(D):
            acc[slot, :, pl.ds(p * HW, HW)] = taps(t, k, m, p, inner(p))

    def rows_of(total):
        for h in range(H):
            y = total[:, h * W : (h + 1) * W]
            left = jnp.where(lane_no == 0, 0.0, pltpu.roll(y[:C], 1, 1))
            right = jnp.where(lane_no == W - 1, 0.0, pltpu.roll(y[2 * C :], W - 1, 1))
            yield h, y[C : 2 * C] + left + right

    def conv_finish(t, k, m, slot):
        for p in range(D):
            total = acc[slot, :, pl.ds(p * HW, HW)]
            if outer(p):
                total += taps(t, k, m, p, outer(p))
            for h, out in rows_of(total):
                yield p * H + h, out

    def conv_whole(t, k, m):
        for p in range(D):
            for h, out in rows_of(taps(t, k, m, p, range(3))):
                yield p * H + h, out

    def conv_plane(t, k, m, p):
        yield from rows_of(taps(t, k, m, p, range(3)))

    def widen(j, r, v):
        at = pl.ds(r * W, W)
        g3[j, 0:C, at] = jnp.where(lane_no == W - 1, 0.0, pltpu.roll(v, W - 1, 1)).astype(bf16)
        g3[j, C : 2 * C, at] = v.astype(bf16)
        g3[j, 2 * C : 3 * C, at] = jnp.where(lane_no == 0, 0.0, pltpu.roll(v, 1, 1)).astype(bf16)

    def wgrad(t, k, j):
        total = None
        for p in range(D):
            lhs = jnp.concatenate([tall(t, k, p + a - 1) for a in range(3)], axis=0)
            part = lax.dot_general(
                lhs, g3[j, :, pl.ds(p * HW, HW)], (((1,), (1,)), ((), ())),
                preferred_element_type=f32,
            )
            total = part if total is None else total + part
        if t == 0:
            dsum[j] = total
            return
        total += dsum[j]
        total = jnp.concatenate([total, jnp.zeros((9 * C, LW - 3 * C), f32)], axis=1)
        for q in range(n):
            for ab in range(9):
                dpart[j, q, ab] = total[ab * C + q * cs : ab * C + (q + 1) * cs]
        for q in range(1, n):
            share(j, q).start()

    def share(j, q):
        target = lax.rem(slab + q, n)
        return pltpu.make_async_remote_copy(
            src_ref=dpart.at[j, target], dst_ref=dgot.at[j, q],
            send_sem=d_s.at[j, q], recv_sem=d_r.at[j, q],
            device_id={"slab": target}, device_id_type=MESH,
        )

    def keep(t, k, r, value):
        held = value.astype(bf16)
        made[t, k, :, pl.ds(r * W, W)] = held
        wide = held.astype(f32)
        if t == 1:
            stage[k, pl.ds(r, C, stride=DH), :] = wide
        return wide

    def hand_on(k):
        src = made.at[0, k]
        if k <= X2:
            @pl.when(has_next)
            def _():
                to_seg(k).start()
                if k == Y2:
                    edge_start(src, X2, next_seg, 0)

            @pl.when(is_last)
            def _():
                edge_start(src, O1 + k, seg, 1)
                second[O1 + k] = made[0, k]
        else:
            @pl.when(has_prev)
            def _():
                to_seg(k).start()
                edge_start(src, k, prev_seg, 0)

    def give_out(k):
        nat[k] = stage[k].astype(bf16)
        if k < R1:
            own_out(k).start()

            @pl.when(is_last)
            def _():
                last_act(k).start()
        else:
            @pl.when(has_prev)
            def _():
                out_prev(k).start()

    def arrived(k):
        @pl.when(has_prev if k <= X2 else has_next)
        def _():
            to_seg(k).wait_recv()

    def edge_arrived(k, side):
        edge_copy(made.at[0, k], k, side, seg, 0).wait_recv()

    load_pair(0, G1, bgrad)
    for r in range(DH):
        put(0, PD, r, staged(G2, r))
    peers = has_prev.astype(jnp.int32) + has_next.astype(jnp.int32) + n - 1
    pl.semaphore_wait(barrier, peers)
    halo_start(0, PD)

    @pl.when(has_prev)
    def _():
        pl.semaphore_signal(
            ready_s.at[1], inc=1, device_id={"segment": prev_seg}, device_id_type=MESH
        )

    @pl.when(has_next)
    def _():
        pl.semaphore_signal(
            ready_s.at[0], inc=1, device_id={"segment": next_seg}, device_id_type=MESH
        )

    load_pair(1, O1, bout)
    for r in range(DH):
        put(0, PH, r, silu(staged(O1, r)))
    halo_start(0, PH)
    load_pair(2, X1, fwd)
    for r in range(DH):
        put(0, PX, r, silu(staged(X2, r)))
    halo_start(0, PX)
    prepare_weights()
    conv_local(0, PD, GT, 0)
    conv_local(0, PH, G, 1)
    conv_local(0, PX, F, 2)
    for r in range(DH):
        widen(1, r, staged(G2, r))

    fetches[4].wait()
    fetches[5].wait()

    @pl.when(is_first)
    def _():
        for s in range(2):
            load_stage(6 + s, nxt, s)
            for r in range(DH):
                second[X1 + s, :, pl.ds(r * W, W)] = staged(6 + s, r).astype(bf16)
        edge_start(second.at[X2], X2, seg, 1)

    @pl.when(is_last)
    def _():
        for s in range(2):
            last_grad(s).start()
            load_stage(6 + s, loss, s)
            for r in range(DH):
                second[G1 + s, :, pl.ds(r * W, W)] = staged(6 + s, r).astype(bf16)
            edge_start(second.at[G1 + s], G1 + s, seg, 1)

    @pl.when(has_prev)
    def _():
        pl.semaphore_wait(ready_s.at[0], 1)

    @pl.when(has_next)
    def _():
        pl.semaphore_wait(ready_s.at[1], 1)

    halo_arrived(0, PD)
    for r, out in conv_finish(0, PD, GT, 0):
        put(0, PE, r, keep(0, E1, r, staged(G1, r) + slope(staged(O1, r)) * out))
    halo_start(0, PE)
    hand_on(E1)
    halo_arrived(0, PH)
    for r, out in conv_finish(0, PH, G, 1):
        put(0, PU, r, silu(keep(0, R2, r, staged(O2, r) - out)))
    halo_start(0, PU)
    hand_on(R2)
    halo_arrived(0, PX)
    for r, out in conv_finish(0, PX, F, 2):
        put(0, PY, r, silu(keep(0, Y1, r, staged(X1, r) + out)))
    halo_start(0, PY)
    hand_on(Y1)

    conv_local(0, PE, FT, 0)
    conv_local(0, PU, F, 1)
    conv_local(0, PY, G, 2)
    wgrad(0, PH, 1)
    for r in range(DH):
        widen(0, r, made[0, E1, :, pl.ds(r * W, W)].astype(f32))

    halo_arrived(0, PE)
    for r, out in conv_finish(0, PE, FT, 0):
        v = made[0, R2, :, pl.ds(r * W, W)].astype(f32)
        keep(0, E2, r, staged(G2, r) + slope(v) * out)
    hand_on(E2)
    halo_arrived(0, PU)
    for r, out in conv_finish(0, PU, F, 1):
        keep(0, R1, r, staged(O1, r) - out)
    hand_on(R1)
    halo_arrived(0, PY)
    for r, out in conv_finish(0, PY, G, 2):
        keep(0, Y2, r, staged(X2, r) + out)
    hand_on(Y2)
    wgrad(0, PU, 0)

    def got(k, r):
        return second[k, :, pl.ds(r * W, W)].astype(f32)

    def near(k, side, h):
        return edge[k, side, :, pl.ds((HW if side == 0 else 0) + h * W, W)].astype(f32)

    def edge_q(side, j):
        return -2 + j if side == 0 else D + j

    arrived(G2)
    for d in range(D):
        pad[1, PD, :, pl.ds(lane(d, 1), HW)] = second[G2, :, pl.ds(d * HW, HW)]
    conv_local(1, PD, GT, 0)
    for r in range(DH):
        widen(1, r, got(G2, r))
    arrived(O1)
    for r in range(DH):
        put(1, PH, r, silu(got(O1, r)))
    conv_local(1, PH, G, 1)

    for side, there in by_side(False):
        @pl.when(there)
        def _():
            edge_arrived(G2, side)
            for j in range(2):
                pad[1, PD, :, pl.ds(lane(edge_q(side, j), 1), HW)] = (
                    edge[G2, side, :, pl.ds(j * HW, HW)]
                )
            edge_arrived(O1, side)
            for j in range(2):
                for h in range(H):
                    v = edge[O1, side, :, pl.ds((j * H + h) * W, W)].astype(f32)
                    pad[1, PH, :, pl.ds(lane(edge_q(side, j), h + 1), W)] = silu(v).astype(bf16)

    arrived(G1)
    for r, out in conv_finish(1, PD, GT, 0):
        put(1, PE, r, keep(1, E1, r, got(G1, r) + slope(got(O1, r)) * out))
    arrived(O2)
    for r, out in conv_finish(1, PH, G, 1):
        put(1, PU, r, silu(keep(1, R2, r, got(O2, r) - out)))

    for side, there in by_side(False):
        @pl.when(there)
        def _():
            p = -1 if side == 0 else D
            edge_arrived(G1, side)
            for h, out in conv_plane(1, PD, GT, p):
                value = near(G1, side, h) + slope(near(O1, side, h)) * out
                pad[1, PE, :, pl.ds(lane(p, h + 1), W)] = value.astype(bf16)
            edge_arrived(O2, side)
            for h, out in conv_plane(1, PH, G, p):
                value = (near(O2, side, h) - out).astype(bf16).astype(f32)
                pad[1, PU, :, pl.ds(lane(p, h + 1), W)] = silu(value).astype(bf16)

    for r, out in conv_whole(1, PE, FT):
        v = made[1, R2, :, pl.ds(r * W, W)].astype(f32)
        keep(1, E2, r, got(G2, r) + slope(v) * out)
    give_out(E2)
    for r, out in conv_whole(1, PU, F):
        keep(1, R1, r, got(O1, r) - out)
    give_out(R1)
    give_out(E1)
    give_out(R2)
    for r in range(DH):
        widen(0, r, made[1, E1, :, pl.ds(r * W, W)].astype(f32))
    wgrad(1, PU, 0)

    arrived(X2)
    for r in range(DH):
        put(1, PX, r, silu(got(X2, r)))
    for side, there in by_side(False):
        @pl.when(there)
        def _():
            edge_arrived(X2, side)
            q = -1 if side == 0 else D
            for h in range(H):
                pad[1, PX, :, pl.ds(lane(q, h + 1), W)] = silu(near(X2, side, h)).astype(bf16)
    arrived(X1)
    for r, out in conv_whole(1, PX, F):
        put(1, PY, r, silu(keep(1, Y1, r, got(X1, r) + out)))
    halo_start(1, PY)
    give_out(Y1)
    conv_local(1, PY, G, 2)
    wgrad(1, PH, 1)

    halo_arrived(1, PY)
    for r, out in conv_finish(1, PY, G, 2):
        keep(1, Y2, r, got(X2, r) + out)
    give_out(Y2)

    for j in (0, 1):
        for q in range(1, n):
            share(j, q).wait_recv()
        total = dpart[j, slab]
        for q in range(1, n):
            total += dgot[j, q]
        total *= scale
        for ab in range(9):
            for c in range(3):
                tap = total[ab] if c == 0 else pltpu.roll(total[ab], LW - c * C, 1)
                dt[j, pl.ds(3 * ab + c, cs, stride=27), :] = tap
        dw[j] = dt[j].T[:C]

    for k in range(6):
        halo_sent(0, k)
    halo_sent(1, PY)
    for j in range(2):
        for q in range(1, n):
            share(j, q).wait_send()
    for k in (Y1, Y2):
        own_out(k).wait()

    @pl.when(is_first)
    def _():
        edge_sent(second.at[X2], X2, seg, 1)

    @pl.when(is_last)
    def _():
        for k in (Y1, Y2):
            last_act(k).wait()
            last_grad(k).wait()
            edge_sent(made.at[0, k], O1 + k, seg, 1)
            edge_sent(second.at[G1 + k], G1 + k, seg, 1)

    @pl.when(has_next)
    def _():
        for k in (Y1, Y2):
            to_seg(k).wait_send()
        edge_sent(made.at[0, Y2], X2, next_seg, 0)
        for k in (R1, R2, E1, E2):
            out_prev(k).wait_recv()

    @pl.when(has_prev)
    def _():
        for k in (R1, R2, E1, E2):
            to_seg(k).wait_send()
            edge_sent(made.at[0, k], k, prev_seg, 0)
            out_prev(k).wait_send()


def write_out(*refs):
    srcs, dsts, sems = refs[:4], refs[4:8], refs[8]
    writes = [pltpu.make_async_copy(a, b, sems.at[i]) for i, (a, b) in enumerate(zip(srcs, dsts))]
    for write in writes:
        write.start()
    for write in writes:
        write.wait()


def local(segs, n, fwd_in, back_out, back_grad, batch_next, loss_grad, weights):
    _, _, C, D, H, W = fwd_in.shape
    rows = C * D * H
    cs = C // n
    f32, bf16 = jnp.float32, jnp.bfloat16
    scale = float(D * n * H * W) ** (-0.5)
    vmem = pl.BlockSpec(memory_space=pltpu.VMEM)
    hbm = pl.BlockSpec(memory_space=pltpu.HBM)
    wide = pl.cdiv(3 * C, 128) * 128
    anywhere = pl.BlockSpec(memory_space=pl.ANY)
    pair = jax.ShapeDtypeStruct((2, rows, W), bf16)
    share = jax.ShapeDtypeStruct((2, C, 27 * cs), f32)
    dma = pltpu.SemaphoreType.DMA
    fout, backs, grads, dw = pl.pallas_call(
        functools.partial(kernel, (C, D, H, W, segs, n, scale)),
        out_shape=tuple(pltpu.VMEM(x.shape, x.dtype) for x in (pair, pair, pair, share)),
        in_specs=[hbm] * 6,
        out_specs=(vmem, vmem, vmem, vmem),
        scratch_shapes=[
            pltpu.VMEM((2, rows, W), bf16),
            pltpu.VMEM((2, rows, W), bf16),
            pltpu.VMEM((2, rows, W), bf16),
            pltpu.VMEM((2, rows, W), bf16),
            pltpu.VMEM((4, rows, W), bf16),
            pltpu.VMEM((2 * C, 27 * C), bf16),
            pltpu.VMEM((27 * C, wide), f32),
            pltpu.VMEM((4, 3, 3 * C, 3 * C), bf16),
            pltpu.VMEM((2, 27 * cs, wide), f32),
            pltpu.VMEM((2, 6, C, (D + 4) * (H + 2) * W), bf16),
            pltpu.VMEM((8, rows, W), f32),
            pltpu.VMEM((6, C, D * H * W), bf16),
            pltpu.VMEM((6, 2, C, 2 * H * W), bf16),
            pltpu.VMEM((2, 6, C, D * H * W), bf16),
            pltpu.VMEM((6, rows, W), bf16),
            pltpu.VMEM((3, 3 * C, D * H * W), f32),
            pltpu.VMEM((2, 3 * C, D * H * W), bf16),
            pltpu.VMEM((2, 9 * C, 3 * C), f32),
            pltpu.VMEM((2, n, 9, cs, wide), f32),
            pltpu.VMEM((2, n, 9, cs, wide), f32),
            dma((2, 6, 2)),
            dma((2, 6, 2)),
            dma((2, 6)),
            dma((2, 6)),
            dma((2, 6, 2)),
            dma((6, 2)),
            dma((6,)),
            dma((2, n)),
            dma((2, n)),
            dma((6,)),
            pltpu.SemaphoreType.REGULAR((2,)),
        ],
        compiler_params=pltpu.CompilerParams(
            collective_id=0, has_side_effects=True, vmem_limit_bytes=48 << 20
        ),
        name="petra",
    )(
        *[
            pltpu.with_memory_space_constraint(x, pltpu.HBM)
            for x in (
                fwd_in.reshape(2, rows, W),
                back_out.reshape(2, rows, W),
                back_grad.reshape(2, rows, W),
                batch_next.reshape(2, rows, W),
                loss_grad.reshape(4, rows, W),
                weights.reshape(2 * C, 27 * C),
            )
        ]
    )
    fout, backs, grads, dw = pl.pallas_call(
        write_out,
        out_shape=(pair, pair, pair, share),
        in_specs=[vmem] * 4,
        out_specs=(hbm,) * 4,
        scratch_shapes=[dma((4,))],
        compiler_params=pltpu.CompilerParams(vmem_limit_bytes=4 << 20),
        name="write_out",
    )(fout, backs, grads, dw)
    shape = fwd_in.shape
    return fout.reshape(shape), backs.reshape(shape), grads.reshape(shape), dw[None]


def solution(mesh):
    field = P("segment", None, None, "slab", None, None)
    return jax.shard_map(
        functools.partial(local, mesh.shape["segment"], mesh.shape["slab"]),
        mesh=mesh,
        in_specs=(
            field,
            field,
            field,
            P(None, None, "slab", None, None),
            P(None, None, None, "slab", None, None),
            P("segment", None, None, None),
        ),
        out_specs=(field, field, field, P("segment", None, None, "slab")),
        check_vma=False,
    )
```

time: 25.2 us -> 24.8 us (0.984); the launches traced: 24.8 us -> 24.7 us
  no operation moved by 1% of the time
where the time goes in v2:
time: 24.8 us; the launch traced here: 24.7 us
  Pallas kernels  24 us (97%)
  between operations  0.64 us (3%)
    pallas_call x1, Pallas kernels, local(): pl.pallas_call(functools.partial(kernel, (C, D, H, W, segs, n, scale)), o...  23.2 us
    pallas_call x1, Pallas kernels, local(): pl.pallas_call(write_out, out_shape=(pair, pair, pair, share), in_specs=[...  0.82 us

profile of v2, /device:TPU:1, one launch (start us, length us, event | category | flops | bytes accessed | tf_op | source)
XLA Modules:
  0.0 24.7 jit_solution(14614346494062415384)
XLA Ops:
  0.6 23.2 %petra.1 = (bf16[2,256,128]{2,1,0:T(8,128)(2,1)S(1)}, bf16[2,256,128]{2,1,0:T(8,128)(2,1)S(1)}, bf16[2,256,128]{2,1,0:T(8,128)(2,1)S(1)}, f32[2,32,432]{2,1,0:T(8,128)S(1)}) custom-call(bf16[2,256,128]{2,1,0:T(8,128)(2,1)} %bitcast.11, bf16[2,256,128]{2,1,0:T(8,128)(2,1)} %bitcast.12, bf16[2,256,128]{2,1,0:T(8,128)(2,1)} %bitcast.13, ...), custom_call_target="tpu_custom_call" | custom-call | tf_op jit(solution)/shard_map/petra/pallas_call | solution.py:607
  23.9 0.8 %write_out.1 = (bf16[2,256,128]{2,1,0:T(8,128)(2,1)}, bf16[2,256,128]{2,1,0:T(8,128)(2,1)}, bf16[2,256,128]{2,1,0:T(8,128)(2,1)}, f32[2,32,432]{2,1,0:T(8,128)}) custom-call(bf16[2,256,128]{2,1,0:T(8,128)(2,1)S(1)} %get-tuple-element.12.refs_0_, bf16[2,256,128]{2,1,0:T(8,128)(2,1)S(1)} %get-tuple-element.13.refs_1_, ...), custom_call_target="tpu_custom_call" | custom-call | tf_op jit(solution)/shard_map/write_out/pallas_call | solution.py:662

commit v3 on v2

v3 whole, which is shorter than its diff:
```python
import functools

import jax
import jax.numpy as jnp
from jax import lax
from jax.experimental import pallas as pl
from jax.experimental.pallas import tpu as pltpu
from jax.sharding import PartitionSpec as P

MESH = pl.DeviceIdType.MESH
F, G, FT, GT = range(4)
X1, X2, O1, O2, G1, G2 = range(6)
Y1, Y2, R1, R2, E1, E2 = range(6)
PX, PH, PD, PY, PU, PE = range(6)


def sigmoid(v):
    return 1.0 / (1.0 + jnp.exp(-v))


def silu(v):
    return v / (1.0 + jnp.exp(-v))


def slope(v):
    sig = sigmoid(v)
    return sig * (1.0 + v * (1.0 - sig))


def kernel(
    dims, fwd_hbm, bout_hbm, bgrad_hbm, nxt_hbm, loss_hbm, kern_hbm, fout, backs, grads, dw,
    fwd, bout, bgrad, nxt, loss, kern, kt, w, dt, pad, stage, second, edge, rest, made, nat, acc,
    g3, dsum, dpart, dgot, halo_s, halo_r, seg_s, seg_r, back_s, back_r, edge_s, edge_r, pass_s,
    out_s, d_s, d_r, in_s, ready_s,
):
    C, D, H, W, segs, n, scale = dims
    DH, HW = D * H, H * W
    cs = C // n
    LW = pl.cdiv(3 * C, 128) * 128
    f32, bf16 = jnp.float32, jnp.bfloat16
    seg = lax.axis_index("segment")
    slab = lax.axis_index("slab")
    has_prev, has_next = seg > 0, seg < segs - 1
    is_first, is_last = seg == 0, seg == segs - 1
    prev_seg = lax.rem(seg + segs - 1, segs)
    next_seg = lax.rem(seg + 1, segs)
    lane_no = lax.broadcasted_iota(jnp.int32, (C, W), 1)

    if n == 2:
        sides = [(None, 1 - slab, 0, 1 - slab)]
        toward = [(None, slab, 0, 1 - slab)]
    else:
        below, above = lax.rem(slab + n - 1, n), lax.rem(slab + 1, n)
        sides = [(slab > 0, 0, 0, below), (slab < n - 1, 1, 1, above)]
        toward = [(slab < n - 1, 0, 0, above), (slab > 0, 1, 1, below)]

    def over(rows, act):
        for there, side, slot, peer in rows:
            if there is None:
                act(side, slot, peer)
            else:
                pl.when(there)(functools.partial(act, side, slot, peer))

    def near_q(side):
        return side * (D + 1) - 1

    barrier = pltpu.get_barrier_semaphore()

    for k in range(1, n):
        pl.semaphore_signal(
            barrier, inc=1, device_id={"slab": lax.rem(slab + k, n)}, device_id_type=MESH
        )

    @pl.when(has_prev)
    def _():
        pl.semaphore_signal(barrier, inc=1, device_id={"segment": prev_seg}, device_id_type=MESH)

    @pl.when(has_next)
    def _():
        pl.semaphore_signal(barrier, inc=1, device_id={"segment": next_seg}, device_id_type=MESH)

    fetches = [
        pltpu.make_async_copy(src, dst, in_s.at[i])
        for i, (src, dst) in enumerate(
            [
                (bgrad_hbm, bgrad), (bout_hbm, bout), (fwd_hbm, fwd),
                (kern_hbm, kern), (nxt_hbm, nxt), (loss_hbm, loss),
            ]
        )
    ]
    for fetch in fetches:
        fetch.start()

    def lanes(at, size):
        return pl.ds(at if isinstance(at, int) else pl.multiple_of(at, W), size)

    def lane(q, hh):
        return ((q + 2) * (H + 2) + hh) * W

    zero = jnp.zeros((C, W), bf16)
    for t in range(2):
        for k in range(6):
            reach = 2 if t == 1 and k in (PH, PD) else 1
            for q in range(-reach, D + reach):
                for hh in (0, H + 1):
                    pad[t, k, :, pl.ds(lane(q, hh), W)] = zero

    for q, missing in ((-1, slab == 0), (D, slab == n - 1)):
        @pl.when(missing)
        def _():
            for t in range(2):
                for k in range(6):
                    pad[t, k, :, pl.ds(lane(q, 1), HW)] = jnp.zeros((C, HW), bf16)

    def load_stage(slot, ref, s):
        stage[slot] = ref[s].astype(f32)

    def staged(slot, r):
        return stage[slot, pl.ds(r, C, stride=DH), :]

    def prepare_weights():
        fetches[3].wait()
        wide = kern[...].astype(f32)
        kt[...] = jnp.concatenate([wide, jnp.zeros((LW - 2 * C, 27 * C), f32)], axis=0).T

        def tap(t):
            return kt[pl.ds(t, C, stride=27), :]

        for a in range(3):
            for c in range(3):
                block = jnp.concatenate([tap(9 * a + 3 * b + c) for b in range(3)], axis=0).T
                for f in range(2):
                    w[F + f, a, c * C : (c + 1) * C, :] = block[f * C : (f + 1) * C].astype(bf16)
                for f in range(2):
                    turned = jnp.concatenate(
                        [
                            tap(9 * (2 - a) + 3 * (2 - b) + 2 - c)[:, f * C : (f + 1) * C]
                            for b in range(3)
                        ],
                        axis=1,
                    )
                    w[FT + f, a, c * C : (c + 1) * C, :] = turned.astype(bf16)

    def load_pair(i, slot, ref):
        fetches[i].wait()
        for s in range(2):
            load_stage(slot + s, ref, s)

    def halo(t, k, side, slot, peer):
        if k == PU:
            src = made.at[t, R2, :, lanes((1 - side) * (D - 1) * HW, HW)]
            dst = rest.at[slot]
        else:
            src = pad.at[t, k, :, lanes(lane((1 - side) * (D - 1), 1), HW)]
            dst = pad.at[t, k, :, lanes(lane(near_q(side), 1), HW)]
        return pltpu.make_async_remote_copy(
            src_ref=src, dst_ref=dst, send_sem=halo_s.at[slot], recv_sem=halo_r.at[6 if t else k, slot],
            device_id={"slab": peer}, device_id_type=MESH,
        )

    def halo_start(t, k):
        over(toward, lambda side, slot, peer: halo(t, k, side, slot, peer).start())

    def halo_arrived(t, k):
        over(sides, lambda side, slot, peer: halo(t, k, side, slot, peer).wait_recv())

    def to_seg(k):
        return pltpu.make_async_remote_copy(
            src_ref=made.at[0, k], dst_ref=second.at[k],
            send_sem=seg_s.at[1 if k <= X2 else 0], recv_sem=seg_r.at[k],
            device_id={"segment": next_seg if k <= X2 else prev_seg}, device_id_type=MESH,
        )

    def edge_part(k, side, slot):
        planes = 2 if k in (O1, G2) else 1
        return planes, edge.at[k, slot, :, lanes((2 - planes) * (1 - side) * HW, planes * HW)]

    def edge_copy(src, k, target, which, side, slot, peer):
        planes, dst = edge_part(k, side, slot)
        return pltpu.make_async_remote_copy(
            src_ref=src.at[:, lanes((1 - side) * (D - planes) * HW, planes * HW)], dst_ref=dst,
            send_sem=edge_s.at[which, slot], recv_sem=edge_r.at[k - 1, slot],
            device_id={"segment": target, "slab": peer}, device_id_type=MESH,
        )

    def edge_start(src, k, target, which):
        over(toward, lambda *side: edge_copy(src, k, target, which, *side).start())

    def edge_arrived(k, side, slot, peer):
        edge_copy(made.at[0, k], k, seg, 0, side, slot, peer).wait_recv()

    def pass_on(k, side, slot, peer):
        if k == G1:
            src = pad.at[0, PE, :, lanes(lane(near_q(side), 1), HW)]
        else:
            src = rest.at[slot]
        return pltpu.make_async_remote_copy(
            src_ref=src, dst_ref=edge_part(k, side, slot)[1],
            send_sem=pass_s.at[slot], recv_sem=edge_r.at[k - 1, slot],
            device_id={"segment": prev_seg}, device_id_type=MESH,
        )

    def pass_start(k):
        @pl.when(has_prev)
        def _():
            over(sides, lambda *side: pass_on(k, *side).start())

    def drain(sem, src):
        pltpu.make_async_remote_copy(
            src_ref=src, dst_ref=src, send_sem=sem, recv_sem=sem,
            device_id={"slab": lax.rem(slab + 1, n)}, device_id_type=MESH,
        ).wait_send()

    def planes_of(count):
        return pad.at[0, 0, :, pl.ds(0, count * HW)]

    def out_prev(k):
        dst = backs.at[k - R1] if k < E1 else grads.at[k - E1]
        return pltpu.make_async_remote_copy(
            src_ref=nat.at[k], dst_ref=dst, send_sem=back_s.at[0], recv_sem=back_r.at[0],
            device_id={"segment": prev_seg}, device_id_type=MESH,
        )

    def own_out(k):
        return pltpu.make_async_copy(nat.at[k], fout.at[k], out_s.at[0])

    def last_act(k):
        return pltpu.make_async_copy(nat.at[k], backs.at[k], out_s.at[1])

    def last_grad(k):
        return pltpu.make_async_copy(loss.at[2 + k], grads.at[k], out_s.at[1])

    def put(t, k, r, value):
        d, h = divmod(r, H)
        put_at(t, k, d, h, value)

    def put_at(t, k, q, h, value):
        pad[t, k, :, lanes(lane(q, h + 1), W)] = value.astype(bf16)

    def tall(t, k, q):
        return jnp.concatenate([pad[t, k, :, lanes(lane(q, b), HW)] for b in range(3)], axis=0)

    def taps(t, k, m, p, which):
        total = None
        for a in which:
            part = jnp.dot(w[m, a], tall(t, k, p + a - 1), preferred_element_type=f32)
            total = part if total is None else total + part
        return total

    def inner(p):
        return [a for a in range(3) if 0 <= p + a - 1 < D]

    def conv_local(t, k, m, slot):
        for p in range(D):
            acc[slot, :, pl.ds(p * HW, HW)] = taps(t, k, m, p, inner(p))

    def rows_of(total):
        for h in range(H):
            y = total[:, h * W : (h + 1) * W]
            left = jnp.where(lane_no == 0, 0.0, pltpu.roll(y[:C], 1, 1))
            right = jnp.where(lane_no == W - 1, 0.0, pltpu.roll(y[2 * C :], W - 1, 1))
            yield h, y[C : 2 * C] + left + right

    def conv_finish(t, k, m, slot):
        def outer(side, at, peer):
            here = lanes(side * (D - 1) * HW, HW)
            acc[slot, :, here] += jnp.dot(
                w[m, 2 * side], tall(t, k, near_q(side)), preferred_element_type=f32
            )

        over(sides, outer)
        for p in range(D):
            for h, out in rows_of(acc[slot, :, pl.ds(p * HW, HW)]):
                yield p * H + h, out

    def conv_whole(t, k, m):
        for p in range(D):
            for h, out in rows_of(taps(t, k, m, p, range(3))):
                yield p * H + h, out

    def widen(j, r, v):
        at = pl.ds(r * W, W)
        g3[j, 0:C, at] = jnp.where(lane_no == W - 1, 0.0, pltpu.roll(v, W - 1, 1)).astype(bf16)
        g3[j, C : 2 * C, at] = v.astype(bf16)
        g3[j, 2 * C : 3 * C, at] = jnp.where(lane_no == 0, 0.0, pltpu.roll(v, 1, 1)).astype(bf16)

    def product(lhs, j, p):
        return lax.dot_general(
            lhs, g3[j, :, lanes(p * HW, HW)], (((1,), (1,)), ((), ())), preferred_element_type=f32
        )

    def wgrad_inner(t, k, j):
        parts = [None] * 3
        for p in range(D):
            which = inner(p)
            part = product(jnp.concatenate([tall(t, k, p + a - 1) for a in which], axis=0), j, p)
            for i, a in enumerate(which):
                block = part[i * 3 * C : (i + 1) * 3 * C]
                parts[a] = block if parts[a] is None else parts[a] + block
        for a in range(3):
            here = pl.ds(a * 3 * C, 3 * C)
            if t == 0:
                dsum[j, here] = parts[a]
            else:
                dsum[j, here] += parts[a]

    def wgrad_outer(t, k, j):
        def outer(side, slot, peer):
            at = side * 6 * C
            here = pl.ds(at if isinstance(at, int) else pl.multiple_of(at, 8), 3 * C)
            dsum[j, here] += product(tall(t, k, near_q(side)), j, side * (D - 1))

        over(sides, outer)

    def wgrad_share(j):
        total = dsum[j]
        total = jnp.concatenate([total, jnp.zeros((9 * C, LW - 3 * C), f32)], axis=1)
        for q in range(n):
            for ab in range(9):
                dpart[j, q, ab] = total[ab * C + q * cs : ab * C + (q + 1) * cs]
        for q in range(1, n):
            share(j, q).start()

    def share(j, q):
        target = lax.rem(slab + q, n)
        return pltpu.make_async_remote_copy(
            src_ref=dpart.at[j, target], dst_ref=dgot.at[j, q],
            send_sem=d_s.at[q - 1], recv_sem=d_r.at[j, q - 1],
            device_id={"slab": target}, device_id_type=MESH,
        )

    def keep(t, k, r, value):
        held = value.astype(bf16)
        made[t, k, :, pl.ds(r * W, W)] = held
        wide = held.astype(f32)
        if t == 1:
            stage[k, pl.ds(r, C, stride=DH), :] = wide
        return wide

    def hand_on(k):
        src = made.at[0, k]
        if k <= X2:
            @pl.when(has_next)
            def _():
                to_seg(k).start()
                if k == Y2:
                    edge_start(src, X2, next_seg, 1)

            @pl.when(is_last)
            def _():
                edge_start(src, O1 + k, seg, 2)
                second[O1 + k] = made[0, k]
        else:
            @pl.when(has_prev)
            def _():
                to_seg(k).start()
                if k in (O1, G2):
                    edge_start(src, k, prev_seg, 0)

    def give_out(k):
        nat[k] = stage[k].astype(bf16)
        if k < R1:
            own_out(k).start()

            @pl.when(is_last)
            def _():
                last_act(k).start()
        else:
            @pl.when(has_prev)
            def _():
                out_prev(k).start()

    def arrived(k):
        @pl.when(has_prev if k <= X2 else has_next)
        def _():
            to_seg(k).wait_recv()

    load_pair(0, G1, bgrad)
    for r in range(DH):
        put(0, PD, r, staged(G2, r))
    peers = has_prev.astype(jnp.int32) + has_next.astype(jnp.int32) + n - 1
    pl.semaphore_wait(barrier, peers)
    halo_start(0, PD)

    @pl.when(has_prev)
    def _():
        pl.semaphore_signal(
            ready_s.at[1], inc=1, device_id={"segment": prev_seg}, device_id_type=MESH
        )

    @pl.when(has_next)
    def _():
        pl.semaphore_signal(
            ready_s.at[0], inc=1, device_id={"segment": next_seg}, device_id_type=MESH
        )

    load_pair(1, O1, bout)
    for r in range(DH):
        put(0, PH, r, silu(staged(O1, r)))
    halo_start(0, PH)
    load_pair(2, X1, fwd)
    for r in range(DH):
        put(0, PX, r, silu(staged(X2, r)))
    halo_start(0, PX)
    prepare_weights()
    conv_local(0, PD, GT, 0)
    conv_local(0, PH, G, 1)
    conv_local(0, PX, F, 2)
    for r in range(DH):
        widen(1, r, staged(G2, r))
    wgrad_inner(0, PH, 1)

    fetches[4].wait()
    fetches[5].wait()

    @pl.when(is_first)
    def _():
        for s in range(2):
            load_stage(6 + s, nxt, s)
            for r in range(DH):
                second[X1 + s, :, pl.ds(r * W, W)] = staged(6 + s, r).astype(bf16)
        edge_start(second.at[X2], X2, seg, 2)

    @pl.when(is_last)
    def _():
        for s in range(2):
            last_grad(s).start()
            load_stage(6 + s, loss, s)
            for r in range(DH):
                second[G1 + s, :, pl.ds(r * W, W)] = staged(6 + s, r).astype(bf16)
            edge_start(second.at[G1 + s], G1 + s, seg, 2)

    @pl.when(has_prev)
    def _():
        pl.semaphore_wait(ready_s.at[0], 1)

    @pl.when(has_next)
    def _():
        pl.semaphore_wait(ready_s.at[1], 1)

    halo_arrived(0, PD)
    for r, out in conv_finish(0, PD, GT, 0):
        put(0, PE, r, keep(0, E1, r, staged(G1, r) + slope(staged(O1, r)) * out))
    halo_start(0, PE)
    hand_on(E1)
    conv_local(0, PE, FT, 0)
    for r in range(DH):
        widen(0, r, made[0, E1, :, pl.ds(r * W, W)].astype(f32))
    halo_arrived(0, PH)
    for r, out in conv_finish(0, PH, G, 1):
        put(0, PU, r, silu(keep(0, R2, r, staged(O2, r) - out)))
    halo_start(0, PU)
    hand_on(R2)
    conv_local(0, PU, F, 1)
    wgrad_outer(0, PH, 1)
    halo_arrived(0, PX)
    for r, out in conv_finish(0, PX, F, 2):
        put(0, PY, r, silu(keep(0, Y1, r, staged(X1, r) + out)))
    halo_start(0, PY)
    hand_on(Y1)
    conv_local(0, PY, G, 2)
    wgrad_inner(0, PU, 0)

    halo_arrived(0, PE)
    pass_start(G1)
    for r, out in conv_finish(0, PE, FT, 0):
        v = made[0, R2, :, pl.ds(r * W, W)].astype(f32)
        keep(0, E2, r, staged(G2, r) + slope(v) * out)
    hand_on(E2)
    halo_arrived(0, PU)

    def rest_in(side, slot, peer):
        for h in range(H):
            v = rest[slot, :, pl.ds(h * W, W)].astype(f32)
            put_at(0, PU, near_q(side), h, silu(v))

    over(sides, rest_in)
    for r, out in conv_finish(0, PU, F, 1):
        keep(0, R1, r, staged(O1, r) - out)
    hand_on(R1)
    pass_start(O2)
    halo_arrived(0, PY)
    for r, out in conv_finish(0, PY, G, 2):
        keep(0, Y2, r, staged(X2, r) + out)
    hand_on(Y2)
    wgrad_outer(0, PU, 0)

    def got(k, r):
        return second[k, :, pl.ds(r * W, W)].astype(f32)

    def near(k, side, slot, h):
        return edge[k, slot, :, lanes((1 - side) * HW + h * W, W)].astype(f32)

    def forward():
        arrived(X2)
        for r in range(DH):
            put(1, PX, r, silu(got(X2, r)))
        conv_local(1, PX, F, 2)
        arrived(X1)

        def edges(side, slot, peer):
            edge_arrived(X2, side, slot, peer)
            for h in range(H):
                put_at(1, PX, near_q(side), h, silu(near(X2, side, slot, h)))

        over(sides, edges)
        for r, out in conv_finish(1, PX, F, 2):
            put(1, PY, r, silu(keep(1, Y1, r, got(X1, r) + out)))
        halo_start(1, PY)
        give_out(Y1)
        conv_local(1, PY, G, 2)

    odd = lax.rem(seg, 2) == 1
    pl.when(odd)(forward)

    arrived(G2)
    for d in range(D):
        pad[1, PD, :, pl.ds(lane(d, 1), HW)] = second[G2, :, pl.ds(d * HW, HW)]
    conv_local(1, PD, GT, 0)
    for r in range(DH):
        widen(1, r, got(G2, r))
    arrived(O1)
    for r in range(DH):
        put(1, PH, r, silu(got(O1, r)))
    conv_local(1, PH, G, 1)
    wgrad_inner(1, PH, 1)

    def edges_in(side, slot, peer):
        edge_arrived(G2, side, slot, peer)
        for j in range(2):
            pad[1, PD, :, lanes(lane(side * (D + 2) - 2 + j, 1), HW)] = (
                edge[G2, slot, :, pl.ds(j * HW, HW)]
            )
        edge_arrived(O1, side, slot, peer)
        for j in range(2):
            for h in range(H):
                v = edge[O1, slot, :, pl.ds((j * H + h) * W, W)].astype(f32)
                put_at(1, PH, side * (D + 2) - 2 + j, h, silu(v))

    over(sides, edges_in)
    arrived(G1)
    for r, out in conv_finish(1, PD, GT, 0):
        put(1, PE, r, keep(1, E1, r, got(G1, r) + slope(got(O1, r)) * out))
    arrived(O2)
    for r, out in conv_finish(1, PH, G, 1):
        put(1, PU, r, silu(keep(1, R2, r, got(O2, r) - out)))

    def beyond(side, slot, peer):
        edge_arrived(G1, side, slot, peer)
        edge_arrived(O2, side, slot, peer)
        q = near_q(side)
        turned, plain = taps(1, PD, GT, q, range(3)), taps(1, PH, G, q, range(3))
        for h, out in rows_of(turned):
            value = near(G1, side, slot, h) + slope(near(O1, side, slot, h)) * out
            put_at(1, PE, q, h, value)
        for h, out in rows_of(plain):
            value = (near(O2, side, slot, h) - out).astype(bf16).astype(f32)
            put_at(1, PU, q, h, silu(value))

    over(sides, beyond)
    wgrad_outer(1, PH, 1)
    wgrad_share(1)
    for r in range(DH):
        widen(0, r, made[1, E1, :, pl.ds(r * W, W)].astype(f32))
    wgrad_inner(1, PU, 0)
    wgrad_outer(1, PU, 0)
    wgrad_share(0)
    give_out(E1)
    give_out(R2)

    pl.when(jnp.logical_not(odd))(forward)

    for r, out in conv_whole(1, PE, FT):
        v = made[1, R2, :, pl.ds(r * W, W)].astype(f32)
        keep(1, E2, r, got(G2, r) + slope(v) * out)
    give_out(E2)
    for r, out in conv_whole(1, PU, F):
        keep(1, R1, r, got(O1, r) - out)
    give_out(R1)

    halo_arrived(1, PY)
    for r, out in conv_finish(1, PY, G, 2):
        keep(1, Y2, r, got(X2, r) + out)
    give_out(Y2)

    for j in (1, 0):
        for q in range(1, n):
            share(j, q).wait_recv()
        total = dpart[j, slab]
        for q in range(1, n):
            total += dgot[j, q]
        total *= scale
        for ab in range(9):
            for c in range(3):
                tap = total[ab] if c == 0 else pltpu.roll(total[ab], LW - c * C, 1)
                dt[j, pl.ds(3 * ab + c, cs, stride=27), :] = tap
        dw[j] = dt[j].T[:C]

    over(toward, lambda side, slot, peer: drain(halo_s.at[slot], planes_of(7)))
    for q in range(1, n):
        drain(d_s.at[q - 1], dpart.at[:, 0])
    pltpu.make_async_copy(nat.at[pl.ds(Y1, 2)], fout, out_s.at[0]).wait()

    @pl.when(is_first)
    def _():
        over(toward, lambda side, slot, peer: drain(edge_s.at[2, slot], planes_of(1)))

    @pl.when(is_last)
    def _():
        pltpu.make_async_copy(nat.at[pl.ds(0, 4)], nat.at[pl.ds(0, 4)], out_s.at[1]).wait()
        over(toward, lambda side, slot, peer: drain(edge_s.at[2, slot], planes_of(6)))

    @pl.when(has_next)
    def _():
        drain(seg_s.at[1], made.at[0, pl.ds(0, 2)])
        over(toward, lambda side, slot, peer: drain(edge_s.at[1, slot], planes_of(1)))
        drain(back_r.at[0], nat.at[pl.ds(R1, 4)])

    @pl.when(has_prev)
    def _():
        drain(seg_s.at[0], made.at[0, pl.ds(0, 4)])
        over(toward, lambda side, slot, peer: drain(edge_s.at[0, slot], planes_of(4)))
        over(sides, lambda side, slot, peer: drain(pass_s.at[slot], planes_of(2)))
        drain(back_s.at[0], nat.at[pl.ds(R1, 4)])


def write_out(*refs):
    srcs, dsts, sems = refs[:4], refs[4:8], refs[8]
    writes = [pltpu.make_async_copy(a, b, sems.at[i]) for i, (a, b) in enumerate(zip(srcs, dsts))]
    for write in writes:
        write.start()
    for write in writes:
        write.wait()


def local(segs, n, fwd_in, back_out, back_grad, batch_next, loss_grad, weights):
    _, _, C, D, H, W = fwd_in.shape
    rows = C * D * H
    cs = C // n
    ends = 1 if n == 2 else 2
    f32, bf16 = jnp.float32, jnp.bfloat16
    scale = float(D * n * H * W) ** (-0.5)
    vmem = pl.BlockSpec(memory_space=pltpu.VMEM)
    hbm = pl.BlockSpec(memory_space=pltpu.HBM)
    wide = pl.cdiv(3 * C, 128) * 128
    anywhere = pl.BlockSpec(memory_space=pl.ANY)
    pair = jax.ShapeDtypeStruct((2, rows, W), bf16)
    share = jax.ShapeDtypeStruct((2, C, 27 * cs), f32)
    dma = pltpu.SemaphoreType.DMA
    fout, backs, grads, dw = pl.pallas_call(
        functools.partial(kernel, (C, D, H, W, segs, n, scale)),
        out_shape=tuple(pltpu.VMEM(x.shape, x.dtype) for x in (pair, pair, pair, share)),
        in_specs=[hbm] * 6,
        out_specs=(vmem, vmem, vmem, vmem),
        scratch_shapes=[
            pltpu.VMEM((2, rows, W), bf16),
            pltpu.VMEM((2, rows, W), bf16),
            pltpu.VMEM((2, rows, W), bf16),
            pltpu.VMEM((2, rows, W), bf16),
            pltpu.VMEM((4, rows, W), bf16),
            pltpu.VMEM((2 * C, 27 * C), bf16),
            pltpu.VMEM((27 * C, wide), f32),
            pltpu.VMEM((4, 3, 3 * C, 3 * C), bf16),
            pltpu.VMEM((2, 27 * cs, wide), f32),
            pltpu.VMEM((2, 6, C, (D + 4) * (H + 2) * W), bf16),
            pltpu.VMEM((8, rows, W), f32),
            pltpu.VMEM((6, C, D * H * W), bf16),
            pltpu.VMEM((6, ends, C, 2 * H * W), bf16),
            pltpu.VMEM((ends, C, H * W), bf16),
            pltpu.VMEM((2, 6, C, D * H * W), bf16),
            pltpu.VMEM((6, rows, W), bf16),
            pltpu.VMEM((3, 3 * C, D * H * W), f32),
            pltpu.VMEM((2, 3 * C, D * H * W), bf16),
            pltpu.VMEM((2, 9 * C, 3 * C), f32),
            pltpu.VMEM((2, n, 9, cs, wide), f32),
            pltpu.VMEM((2, n, 9, cs, wide), f32),
            dma((ends,)),
            dma((7, ends)),
            dma((2,)),
            dma((6,)),
            dma((1,)),
            dma((1,)),
            dma((3, ends)),
            dma((5, ends)),
            dma((ends,)),
            dma((2,)),
            dma((n - 1,)),
            dma((2, n - 1)),
            dma((6,)),
            pltpu.SemaphoreType.REGULAR((2,)),
        ],
        compiler_params=pltpu.CompilerParams(
            collective_id=0, has_side_effects=True, vmem_limit_bytes=48 << 20
        ),
        name="petra",
    )(
        *[
            pltpu.with_memory_space_constraint(x, pltpu.HBM)
            for x in (
                fwd_in.reshape(2, rows, W),
                back_out.reshape(2, rows, W),
                back_grad.reshape(2, rows, W),
                batch_next.reshape(2, rows, W),
                loss_grad.reshape(4, rows, W),
                weights.reshape(2 * C, 27 * C),
            )
        ]
    )
    fout, backs, grads, dw = pl.pallas_call(
        write_out,
        out_shape=(pair, pair, pair, share),
        in_specs=[vmem] * 4,
        out_specs=(hbm,) * 4,
        scratch_shapes=[dma((4,))],
        compiler_params=pltpu.CompilerParams(vmem_limit_bytes=4 << 20),
        name="write_out",
    )(fout, backs, grads, dw)
    shape = fwd_in.shape
    return fout.reshape(shape), backs.reshape(shape), grads.reshape(shape), dw[None]


def solution(mesh):
    field = P("segment", None, None, "slab", None, None)
    return jax.shard_map(
        functools.partial(local, mesh.shape["segment"], mesh.shape["slab"]),
        mesh=mesh,
        in_specs=(
            field,
            field,
            field,
            P(None, None, "slab", None, None),
            P(None, None, None, "slab", None, None),
            P("segment", None, None, None),
        ),
        out_specs=(field, field, field, P("segment", None, None, "slab")),
        check_vma=False,
    )
```

time: 24.8 us -> 24.5 us (0.988)
  Pallas kernels: 24 us -> 23.7 us
    pallas_call x1, Pallas kernels: 23.2 us -> 22.9 us  [local(): pl.pallas_call(functools.partial(kernel, (C, D, H, W, segs, n, scale)), o...]
where the time goes in v3:
time: 24.5 us; the launch traced here: 24.3 us
  Pallas kernels  23.7 us (97%)
  between operations  0.64 us (3%)
    pallas_call x1, Pallas kernels, local(): pl.pallas_call(functools.partial(kernel, (C, D, H, W, segs, n, scale)), o...  22.9 us
    pallas_call x1, Pallas kernels, local(): pl.pallas_call(write_out, out_shape=(pair, pair, pair, share), in_specs=[...  0.82 us

profile of v3, /device:TPU:1, one launch (start us, length us, event | category | flops | bytes accessed | tf_op | source)
XLA Modules:
  0.0 24.3 jit_solution(2284207585947279467)
XLA Ops:
  0.6 22.9 %petra.1 = (bf16[2,256,128]{2,1,0:T(8,128)(2,1)S(1)}, bf16[2,256,128]{2,1,0:T(8,128)(2,1)S(1)}, bf16[2,256,128]{2,1,0:T(8,128)(2,1)S(1)}, f32[2,32,432]{2,1,0:T(8,128)S(1)}) custom-call(bf16[2,256,128]{2,1,0:T(8,128)(2,1)} %bitcast.11, bf16[2,256,128]{2,1,0:T(8,128)(2,1)} %bitcast.12, bf16[2,256,128]{2,1,0:T(8,128)(2,1)} %bitcast.13, ...), custom_call_target="tpu_custom_call" | custom-call | tf_op jit(solution)/shard_map/petra/pallas_call | solution.py:650
  23.5 0.8 %write_out.1 = (bf16[2,256,128]{2,1,0:T(8,128)(2,1)}, bf16[2,256,128]{2,1,0:T(8,128)(2,1)}, bf16[2,256,128]{2,1,0:T(8,128)(2,1)}, f32[2,32,432]{2,1,0:T(8,128)}) custom-call(bf16[2,256,128]{2,1,0:T(8,128)(2,1)S(1)} %get-tuple-element.12.refs_0_, bf16[2,256,128]{2,1,0:T(8,128)(2,1)S(1)} %get-tuple-element.13.refs_1_, ...), custom_call_target="tpu_custom_call" | custom-call | tf_op jit(solution)/shard_map/write_out/pallas_call | solution.py:709

commit v4 on v3

--- a/solution.py
+++ b/solution.py
@@ -171,23 +171,22 @@
             device_id={"segment": next_seg if k <= X2 else prev_seg}, device_id_type=MESH,
         )
 
-    def edge_part(k, side, slot):
-        planes = 2 if k in (O1, G2) else 1
-        return planes, edge.at[k, slot, :, lanes((2 - planes) * (1 - side) * HW, planes * HW)]
-
-    def edge_copy(src, k, target, which, side, slot, peer):
-        planes, dst = edge_part(k, side, slot)
+    def edge_at(k, far, side, slot):
+        return edge.at[k, slot, :, lanes((side if far else 1 - side) * HW, HW)]
+
+    def edge_copy(src, k, far, target, which, side, slot, peer):
+        plane = (1 - side) * (D - 2) + side if far else (1 - side) * (D - 1)
         return pltpu.make_async_remote_copy(
-            src_ref=src.at[:, lanes((1 - side) * (D - planes) * HW, planes * HW)], dst_ref=dst,
-            send_sem=edge_s.at[which, slot], recv_sem=edge_r.at[k - 1, slot],
+            src_ref=src.at[:, lanes(plane * HW, HW)], dst_ref=edge_at(k, far, side, slot),
+            send_sem=edge_s.at[which, slot], recv_sem=edge_r.at[k // 2 + 4 if far else k - 1, slot],
             device_id={"segment": target, "slab": peer}, device_id_type=MESH,
         )
 
-    def edge_start(src, k, target, which):
-        over(toward, lambda *side: edge_copy(src, k, target, which, *side).start())
-
-    def edge_arrived(k, side, slot, peer):
-        edge_copy(made.at[0, k], k, seg, 0, side, slot, peer).wait_recv()
+    def edge_start(src, k, far, target, which):
+        over(toward, lambda *side: edge_copy(src, k, far, target, which, *side).start())
+
+    def edge_arrived(k, far, *side):
+        edge_copy(made.at[0, k], k, far, seg, 0, *side).wait_recv()
 
     def pass_on(k, side, slot, peer):
         if k == G1:
@@ -195,15 +194,10 @@
         else:
             src = rest.at[slot]
         return pltpu.make_async_remote_copy(
-            src_ref=src, dst_ref=edge_part(k, side, slot)[1],
+            src_ref=src, dst_ref=edge_at(k, False, side, slot),
             send_sem=pass_s.at[slot], recv_sem=edge_r.at[k - 1, slot],
             device_id={"segment": prev_seg}, device_id_type=MESH,
         )
-
-    def pass_start(k):
-        @pl.when(has_prev)
-        def _():
-            over(sides, lambda *side: pass_on(k, *side).start())
 
     def drain(sem, src):
         pltpu.make_async_remote_copy(
@@ -342,20 +336,30 @@
         if k <= X2:
             @pl.when(has_next)
             def _():
+                if k == Y2:
+                    edge_start(src, X2, False, next_seg, 1)
                 to_seg(k).start()
-                if k == Y2:
-                    edge_start(src, X2, next_seg, 1)
 
             @pl.when(is_last)
             def _():
-                edge_start(src, O1 + k, seg, 2)
+                edge_start(src, O1 + k, False, seg, 2)
+                if k == Y1:
+                    edge_start(src, O1, True, seg, 2)
                 second[O1 + k] = made[0, k]
         else:
             @pl.when(has_prev)
             def _():
                 to_seg(k).start()
                 if k in (O1, G2):
-                    edge_start(src, k, prev_seg, 0)
+                    edge_start(src, k, False, prev_seg, 0)
+
+    def hand_on_far():
+        @pl.when(has_prev)
+        def _():
+            for k in (G2, O1):
+                edge_start(made.at[0, k], k, True, prev_seg, 0)
+            for k in (G1, O2):
+                over(sides, lambda *side: pass_on(k, *side).start())
 
     def give_out(k):
         nat[k] = stage[k].astype(bf16)
@@ -419,7 +423,7 @@
             load_stage(6 + s, nxt, s)
             for r in range(DH):
                 second[X1 + s, :, pl.ds(r * W, W)] = staged(6 + s, r).astype(bf16)
-        edge_start(second.at[X2], X2, seg, 2)
+        edge_start(second.at[X2], X2, False, seg, 2)
 
     @pl.when(is_last)
     def _():
@@ -428,7 +432,8 @@
             load_stage(6 + s, loss, s)
             for r in range(DH):
                 second[G1 + s, :, pl.ds(r * W, W)] = staged(6 + s, r).astype(bf16)
-            edge_start(second.at[G1 + s], G1 + s, seg, 2)
+            edge_start(second.at[G1 + s], G1 + s, False, seg, 2)
+        edge_start(second.at[G2], G2, True, seg, 2)
 
     @pl.when(has_prev)
     def _():
@@ -462,7 +467,6 @@
     wgrad_inner(0, PU, 0)
 
     halo_arrived(0, PE)
-    pass_start(G1)
     for r, out in conv_finish(0, PE, FT, 0):
         v = made[0, R2, :, pl.ds(r * W, W)].astype(f32)
         keep(0, E2, r, staged(G2, r) + slope(v) * out)
@@ -478,11 +482,11 @@
     for r, out in conv_finish(0, PU, F, 1):
         keep(0, R1, r, staged(O1, r) - out)
     hand_on(R1)
-    pass_start(O2)
     halo_arrived(0, PY)
     for r, out in conv_finish(0, PY, G, 2):
         keep(0, Y2, r, staged(X2, r) + out)
     hand_on(Y2)
+    hand_on_far()
     wgrad_outer(0, PU, 0)
 
     def got(k, r):
@@ -499,7 +503,7 @@
         arrived(X1)
 
         def edges(side, slot, peer):
-            edge_arrived(X2, side, slot, peer)
+            edge_arrived(X2, False, side, slot, peer)
             for h in range(H):
                 put_at(1, PX, near_q(side), h, silu(near(X2, side, slot, h)))
 
@@ -525,29 +529,32 @@
     conv_local(1, PH, G, 1)
     wgrad_inner(1, PH, 1)
 
-    def edges_in(side, slot, peer):
-        edge_arrived(G2, side, slot, peer)
-        for j in range(2):
-            pad[1, PD, :, lanes(lane(side * (D + 2) - 2 + j, 1), HW)] = (
-                edge[G2, slot, :, pl.ds(j * HW, HW)]
-            )
-        edge_arrived(O1, side, slot, peer)
-        for j in range(2):
-            for h in range(H):
-                v = edge[O1, slot, :, pl.ds((j * H + h) * W, W)].astype(f32)
-                put_at(1, PH, side * (D + 2) - 2 + j, h, silu(v))
-
-    over(sides, edges_in)
+    def edges_in(far, side, slot, peer):
+        q = near_q(side) + (2 * side - 1 if far else 0)
+        at = (side if far else 1 - side) * HW
+        edge_arrived(G2, far, side, slot, peer)
+        pad[1, PD, :, lanes(lane(q, 1), HW)] = edge[G2, slot, :, lanes(at, HW)]
+        edge_arrived(O1, far, side, slot, peer)
+        for h in range(H):
+            put_at(1, PH, q, h, silu(edge[O1, slot, :, lanes(at + h * W, W)].astype(f32)))
+
+    over(sides, functools.partial(edges_in, False))
     arrived(G1)
     for r, out in conv_finish(1, PD, GT, 0):
         put(1, PE, r, keep(1, E1, r, got(G1, r) + slope(got(O1, r)) * out))
     arrived(O2)
     for r, out in conv_finish(1, PH, G, 1):
         put(1, PU, r, silu(keep(1, R2, r, got(O2, r) - out)))
+    wgrad_outer(1, PH, 1)
+    wgrad_share(1)
+    for r in range(DH):
+        widen(0, r, made[1, E1, :, pl.ds(r * W, W)].astype(f32))
+    wgrad_inner(1, PU, 0)
 
     def beyond(side, slot, peer):
-        edge_arrived(G1, side, slot, peer)
-        edge_arrived(O2, side, slot, peer)
+        edges_in(True, side, slot, peer)
+        edge_arrived(G1, False, side, slot, peer)
+        edge_arrived(O2, False, side, slot, peer)
         q = near_q(side)
         turned, plain = taps(1, PD, GT, q, range(3)), taps(1, PH, G, q, range(3))
         for h, out in rows_of(turned):
@@ -558,11 +565,6 @@
             put_at(1, PU, q, h, silu(value))
 
     over(sides, beyond)
-    wgrad_outer(1, PH, 1)
-    wgrad_share(1)
-    for r in range(DH):
-        widen(0, r, made[1, E1, :, pl.ds(r * W, W)].astype(f32))
-    wgrad_inner(1, PU, 0)
     wgrad_outer(1, PU, 0)
     wgrad_share(0)
     give_out(E1)
@@ -681,7 +683,7 @@
             dma((1,)),
             dma((1,)),
             dma((3, ends)),
-            dma((5, ends)),
+            dma((7, ends)),
             dma((ends,)),
             dma((2,)),
             dma((n - 1,)),

time: 24.5 us -> 22.9 us (0.935)
  the two profiles are of different devices: /device:TPU:1 before, /device:TPU:21 now
where the time goes in v4:
time: 22.9 us; the launch traced here: 22.8 us
  Pallas kernels  22.1 us (97%)
  between operations  0.64 us (3%)
    pallas_call x1, Pallas kernels, local(): pl.pallas_call(functools.partial(kernel, (C, D, H, W, segs, n, scale)), o...  21.3 us
    pallas_call x1, Pallas kernels, local(): pl.pallas_call(write_out, out_shape=(pair, pair, pair, share), in_specs=[...  0.82 us

profile of v4, /device:TPU:21, one launch (start us, length us, event | category | flops | bytes accessed | tf_op | source)
XLA Modules:
  0.0 22.8 jit_solution(12473652060145453664)
XLA Ops:
  0.6 21.3 %petra.1 = (bf16[2,256,128]{2,1,0:T(8,128)(2,1)S(1)}, bf16[2,256,128]{2,1,0:T(8,128)(2,1)S(1)}, bf16[2,256,128]{2,1,0:T(8,128)(2,1)S(1)}, f32[2,32,432]{2,1,0:T(8,128)S(1)}) custom-call(bf16[2,256,128]{2,1,0:T(8,128)(2,1)} %bitcast.11, bf16[2,256,128]{2,1,0:T(8,128)(2,1)} %bitcast.12, bf16[2,256,128]{2,1,0:T(8,128)(2,1)} %bitcast.13, ...), custom_call_target="tpu_custom_call" | custom-call | tf_op jit(solution)/shard_map/petra/pallas_call | solution.py:652
  21.9 0.8 %write_out.1 = (bf16[2,256,128]{2,1,0:T(8,128)(2,1)}, bf16[2,256,128]{2,1,0:T(8,128)(2,1)}, bf16[2,256,128]{2,1,0:T(8,128)(2,1)}, f32[2,32,432]{2,1,0:T(8,128)}) custom-call(bf16[2,256,128]{2,1,0:T(8,128)(2,1)S(1)} %get-tuple-element.12.refs_0_, bf16[2,256,128]{2,1,0:T(8,128)(2,1)S(1)} %get-tuple-element.13.refs_1_, ...), custom_call_target="tpu_custom_call" | custom-call | tf_op jit(solution)/shard_map/write_out/pallas_call | solution.py:711

commit v5 on v4

--- a/solution.py
+++ b/solution.py
@@ -42,6 +42,9 @@
     slab = lax.axis_index("slab")
     has_prev, has_next = seg > 0, seg < segs - 1
     is_first, is_last = seg == 0, seg == segs - 1
+    odd, even = lax.rem(seg, 2) == 1, lax.rem(seg, 2) == 0
+    relayed = jnp.logical_and(has_next, odd)
+    whole = jnp.logical_and(has_next, even)
     prev_seg = lax.rem(seg + segs - 1, segs)
     next_seg = lax.rem(seg + 1, segs)
     lane_no = lax.broadcasted_iota(jnp.int32, (C, W), 1)
@@ -255,17 +258,24 @@
             right = jnp.where(lane_no == W - 1, 0.0, pltpu.roll(y[2 * C :], W - 1, 1))
             yield h, y[C : 2 * C] + left + right
 
-    def conv_finish(t, k, m, slot):
-        def outer(side, at, peer):
-            here = lanes(side * (D - 1) * HW, HW)
-            acc[slot, :, here] += jnp.dot(
-                w[m, 2 * side], tall(t, k, near_q(side)), preferred_element_type=f32
-            )
-
-        over(sides, outer)
-        for p in range(D):
-            for h, out in rows_of(acc[slot, :, pl.ds(p * HW, HW)]):
-                yield p * H + h, out
+    def conv_finish(t, k, m, slot, act, then=None):
+        def outer(side):
+            return jnp.dot(w[m, 2 * side], tall(t, k, near_q(side)), preferred_element_type=f32)
+
+        def add(side, at, peer):
+            acc[slot, :, lanes(side * (D - 1) * HW, HW)] += outer(side)
+
+        if n > 2:
+            over(sides, add)
+        for i in range(D):
+            p = (1 - slab) * (D - 1) + i * (2 * slab - 1) if n == 2 else i
+            total = acc[slot, :, lanes(p * HW, HW)]
+            if n == 2 and i == 0:
+                total += outer(1 - slab)
+            for h, out in rows_of(total):
+                act(p * H + h, p, h, out)
+            if then is not None and i == (0 if n == 2 else D - 1):
+                then()
 
     def conv_whole(t, k, m):
         for p in range(D):
@@ -298,6 +308,13 @@
             else:
                 dsum[j, here] += parts[a]
 
+    def wgrad_whole(k, j):
+        for p in range(D):
+            lhs = jnp.concatenate([tall(1, k, p + a - 1) for a in range(3)], axis=0)
+            part = product(lhs, j, p)
+            total = part if p == 0 else total + part
+        dsum[j] += total
+
     def wgrad_outer(t, k, j):
         def outer(side, slot, peer):
             at = side * 6 * C
@@ -307,25 +324,26 @@
         over(sides, outer)
 
     def wgrad_share(j):
-        total = dsum[j]
-        total = jnp.concatenate([total, jnp.zeros((9 * C, LW - 3 * C), f32)], axis=1)
-        for q in range(n):
+        for q in range(1, n):
+            first = lax.rem(slab + q, n) * cs
             for ab in range(9):
-                dpart[j, q, ab] = total[ab * C + q * cs : ab * C + (q + 1) * cs]
-        for q in range(1, n):
+                part = dsum[j, pl.ds(pl.multiple_of(ab * C + first, 8), cs)].astype(bf16)
+                dpart[j, q - 1, ab] = jnp.concatenate(
+                    [part, jnp.zeros((cs, LW - 3 * C), bf16)], axis=1
+                )
             share(j, q).start()
 
     def share(j, q):
         target = lax.rem(slab + q, n)
         return pltpu.make_async_remote_copy(
-            src_ref=dpart.at[j, target], dst_ref=dgot.at[j, q],
+            src_ref=dpart.at[j, q - 1], dst_ref=dgot.at[j, q - 1],
             send_sem=d_s.at[q - 1], recv_sem=d_r.at[j, q - 1],
             device_id={"slab": target}, device_id_type=MESH,
         )
 
     def keep(t, k, r, value):
         held = value.astype(bf16)
-        made[t, k, :, pl.ds(r * W, W)] = held
+        made[t, k, :, lanes(r * W, W)] = held
         wide = held.astype(f32)
         if t == 1:
             stage[k, pl.ds(r, C, stride=DH), :] = wide
@@ -350,11 +368,13 @@
             @pl.when(has_prev)
             def _():
                 to_seg(k).start()
-                if k in (O1, G2):
-                    edge_start(src, k, False, prev_seg, 0)
+                if k == O1:
+                    edge_start(src, O1, False, prev_seg, 0)
+                    edge_start(made.at[0, G2], G2, False, prev_seg, 0)
+                    pl.when(even)(functools.partial(edge_start, src, O1, True, prev_seg, 0))
 
     def hand_on_far():
-        @pl.when(has_prev)
+        @pl.when(odd)
         def _():
             for k in (G2, O1):
                 edge_start(made.at[0, k], k, True, prev_seg, 0)
@@ -375,7 +395,9 @@
                 out_prev(k).start()
 
     def arrived(k):
-        @pl.when(has_prev if k <= X2 else has_next)
+        there = has_prev if k <= X2 else whole if k in (G1, O2) else has_next
+
+        @pl.when(there)
         def _():
             to_seg(k).wait_recv()
 
@@ -444,32 +466,41 @@
         pl.semaphore_wait(ready_s.at[1], 1)
 
     halo_arrived(0, PD)
-    for r, out in conv_finish(0, PD, GT, 0):
-        put(0, PE, r, keep(0, E1, r, staged(G1, r) + slope(staged(O1, r)) * out))
-    halo_start(0, PE)
+
+    def act(r, p, h, out):
+        put_at(0, PE, p, h, keep(0, E1, r, staged(G1, r) + slope(staged(O1, r)) * out))
+
+    conv_finish(0, PD, GT, 0, act, functools.partial(halo_start, 0, PE))
     hand_on(E1)
     conv_local(0, PE, FT, 0)
     for r in range(DH):
         widen(0, r, made[0, E1, :, pl.ds(r * W, W)].astype(f32))
     halo_arrived(0, PH)
-    for r, out in conv_finish(0, PH, G, 1):
-        put(0, PU, r, silu(keep(0, R2, r, staged(O2, r) - out)))
-    halo_start(0, PU)
+
+    def act(r, p, h, out):
+        put_at(0, PU, p, h, silu(keep(0, R2, r, staged(O2, r) - out)))
+
+    conv_finish(0, PH, G, 1, act, functools.partial(halo_start, 0, PU))
     hand_on(R2)
     conv_local(0, PU, F, 1)
     wgrad_outer(0, PH, 1)
     halo_arrived(0, PX)
-    for r, out in conv_finish(0, PX, F, 2):
-        put(0, PY, r, silu(keep(0, Y1, r, staged(X1, r) + out)))
-    halo_start(0, PY)
+
+    def act(r, p, h, out):
+        put_at(0, PY, p, h, silu(keep(0, Y1, r, staged(X1, r) + out)))
+
+    conv_finish(0, PX, F, 2, act, functools.partial(halo_start, 0, PY))
     hand_on(Y1)
     conv_local(0, PY, G, 2)
     wgrad_inner(0, PU, 0)
 
     halo_arrived(0, PE)
-    for r, out in conv_finish(0, PE, FT, 0):
-        v = made[0, R2, :, pl.ds(r * W, W)].astype(f32)
+
+    def act(r, p, h, out):
+        v = made[0, R2, :, lanes(r * W, W)].astype(f32)
         keep(0, E2, r, staged(G2, r) + slope(v) * out)
+
+    conv_finish(0, PE, FT, 0, act)
     hand_on(E2)
     halo_arrived(0, PU)
 
@@ -479,27 +510,33 @@
             put_at(0, PU, near_q(side), h, silu(v))
 
     over(sides, rest_in)
-    for r, out in conv_finish(0, PU, F, 1):
-        keep(0, R1, r, staged(O1, r) - out)
+    conv_finish(0, PU, F, 1, lambda r, p, h, out: keep(0, R1, r, staged(O1, r) - out))
     hand_on(R1)
     halo_arrived(0, PY)
-    for r, out in conv_finish(0, PY, G, 2):
-        keep(0, Y2, r, staged(X2, r) + out)
+    conv_finish(0, PY, G, 2, lambda r, p, h, out: keep(0, Y2, r, staged(X2, r) + out))
     hand_on(Y2)
     hand_on_far()
     wgrad_outer(0, PU, 0)
 
     def got(k, r):
-        return second[k, :, pl.ds(r * W, W)].astype(f32)
+        return second[k, :, lanes(r * W, W)].astype(f32)
 
     def near(k, side, slot, h):
         return edge[k, slot, :, lanes((1 - side) * HW + h * W, W)].astype(f32)
 
-    def forward():
+    @pl.when(relayed)
+    def _():
+        for k in (G1, O2):
+            to_seg(k).wait_recv()
+            edge_start(second.at[k], k, False, seg, 3)
+
+    def forward_own():
         arrived(X2)
         for r in range(DH):
             put(1, PX, r, silu(got(X2, r)))
         conv_local(1, PX, F, 2)
+
+    def forward():
         arrived(X1)
 
         def edges(side, slot, peer):
@@ -508,26 +545,32 @@
                 put_at(1, PX, near_q(side), h, silu(near(X2, side, slot, h)))
 
         over(sides, edges)
-        for r, out in conv_finish(1, PX, F, 2):
-            put(1, PY, r, silu(keep(1, Y1, r, got(X1, r) + out)))
-        halo_start(1, PY)
+
+        def act(r, p, h, out):
+            put_at(1, PY, p, h, silu(keep(1, Y1, r, got(X1, r) + out)))
+
+        conv_finish(1, PX, F, 2, act, functools.partial(halo_start, 1, PY))
         give_out(Y1)
         conv_local(1, PY, G, 2)
 
-    odd = lax.rem(seg, 2) == 1
-    pl.when(odd)(forward)
-
     arrived(G2)
+
+    @pl.when(relayed)
+    def _():
+        edge_start(second.at[G2], G2, True, seg, 3)
+
+    pl.when(odd)(forward_own)
     for d in range(D):
         pad[1, PD, :, pl.ds(lane(d, 1), HW)] = second[G2, :, pl.ds(d * HW, HW)]
     conv_local(1, PD, GT, 0)
-    for r in range(DH):
-        widen(1, r, got(G2, r))
     arrived(O1)
     for r in range(DH):
         put(1, PH, r, silu(got(O1, r)))
     conv_local(1, PH, G, 1)
+    for r in range(DH):
+        widen(1, r, got(G2, r))
     wgrad_inner(1, PH, 1)
+    pl.when(odd)(forward)
 
     def edges_in(far, side, slot, peer):
         q = near_q(side) + (2 * side - 1 if far else 0)
@@ -540,16 +583,19 @@
 
     over(sides, functools.partial(edges_in, False))
     arrived(G1)
-    for r, out in conv_finish(1, PD, GT, 0):
-        put(1, PE, r, keep(1, E1, r, got(G1, r) + slope(got(O1, r)) * out))
+
+    def act(r, p, h, out):
+        put_at(1, PE, p, h, keep(1, E1, r, got(G1, r) + slope(got(O1, r)) * out))
+
+    conv_finish(1, PD, GT, 0, act)
     arrived(O2)
-    for r, out in conv_finish(1, PH, G, 1):
-        put(1, PU, r, silu(keep(1, R2, r, got(O2, r) - out)))
-    wgrad_outer(1, PH, 1)
-    wgrad_share(1)
+
+    def act(r, p, h, out):
+        put_at(1, PU, p, h, silu(keep(1, R2, r, got(O2, r) - out)))
+
+    conv_finish(1, PH, G, 1, act)
     for r in range(DH):
         widen(0, r, made[1, E1, :, pl.ds(r * W, W)].astype(f32))
-    wgrad_inner(1, PU, 0)
 
     def beyond(side, slot, peer):
         edges_in(True, side, slot, peer)
@@ -565,12 +611,13 @@
             put_at(1, PU, q, h, silu(value))
 
     over(sides, beyond)
-    wgrad_outer(1, PU, 0)
+    wgrad_whole(PU, 0)
     wgrad_share(0)
+    wgrad_outer(1, PH, 1)
+    wgrad_share(1)
     give_out(E1)
     give_out(R2)
 
-    pl.when(jnp.logical_not(odd))(forward)
 
     for r, out in conv_whole(1, PE, FT):
         v = made[1, R2, :, pl.ds(r * W, W)].astype(f32)
@@ -580,23 +627,31 @@
         keep(1, R1, r, got(O1, r) - out)
     give_out(R1)
 
+    def gradients():
+        for j in (0, 1):
+            for q in range(1, n):
+                share(j, q).wait_recv()
+            for ab in range(9):
+                own = dsum[j, pl.ds(pl.multiple_of(ab * C + slab * cs, 8), cs)]
+                total = jnp.concatenate([own, jnp.zeros((cs, LW - 3 * C), f32)], axis=1)
+                for q in range(1, n):
+                    total += dgot[j, q - 1, ab].astype(f32)
+                total *= scale
+                for c in range(3):
+                    tap = total if c == 0 else pltpu.roll(total, LW - c * C, 1)
+                    dt[j, pl.ds(3 * ab + c, cs, stride=27), :] = tap
+            dw[j] = dt[j].T[:C]
+
+    @pl.when(even)
+    def _():
+        forward_own()
+        forward()
+        gradients()
+
     halo_arrived(1, PY)
-    for r, out in conv_finish(1, PY, G, 2):
-        keep(1, Y2, r, got(X2, r) + out)
+    conv_finish(1, PY, G, 2, lambda r, p, h, out: keep(1, Y2, r, got(X2, r) + out))
     give_out(Y2)
-
-    for j in (1, 0):
-        for q in range(1, n):
-            share(j, q).wait_recv()
-        total = dpart[j, slab]
-        for q in range(1, n):
-            total += dgot[j, q]
-        total *= scale
-        for ab in range(9):
-            for c in range(3):
-                tap = total[ab] if c == 0 else pltpu.roll(total[ab], LW - c * C, 1)
-                dt[j, pl.ds(3 * ab + c, cs, stride=27), :] = tap
-        dw[j] = dt[j].T[:C]
+    pl.when(odd)(gradients)
 
     over(toward, lambda side, slot, peer: drain(halo_s.at[slot], planes_of(7)))
     for q in range(1, n):
@@ -621,9 +676,20 @@
     @pl.when(has_prev)
     def _():
         drain(seg_s.at[0], made.at[0, pl.ds(0, 4)])
+        drain(back_s.at[0], nat.at[pl.ds(R1, 4)])
+
+        @pl.when(even)
+        def _():
+            over(toward, lambda side, slot, peer: drain(edge_s.at[0, slot], planes_of(3)))
+
+    @pl.when(odd)
+    def _():
         over(toward, lambda side, slot, peer: drain(edge_s.at[0, slot], planes_of(4)))
         over(sides, lambda side, slot, peer: drain(pass_s.at[slot], planes_of(2)))
-        drain(back_s.at[0], nat.at[pl.ds(R1, 4)])
+
+    @pl.when(relayed)
+    def _():
+        over(toward, lambda side, slot, peer: drain(edge_s.at[3, slot], planes_of(3)))
 
 
 def write_out(*refs):
@@ -674,15 +740,15 @@
             pltpu.VMEM((3, 3 * C, D * H * W), f32),
             pltpu.VMEM((2, 3 * C, D * H * W), bf16),
             pltpu.VMEM((2, 9 * C, 3 * C), f32),
-            pltpu.VMEM((2, n, 9, cs, wide), f32),
-            pltpu.VMEM((2, n, 9, cs, wide), f32),
+            pltpu.VMEM((2, n - 1, 9, cs, wide), bf16),
+            pltpu.VMEM((2, n - 1, 9, cs, wide), bf16),
             dma((ends,)),
             dma((7, ends)),
             dma((2,)),
             dma((6,)),
             dma((1,)),
             dma((1,)),
-            dma((3, ends)),
+            dma((4, ends)),
             dma((7, ends)),
             dma((ends,)),
             dma((2,)),

time: 22.9 us -> 21.9 us (0.956)
  the two profiles are of different devices: /device:TPU:21 before, /device:TPU:1 now
where the time goes in v5:
time: 21.9 us; the launch traced here: 21.8 us
  Pallas kernels  21.1 us (96%)
  between operations  0.64 us (3%)
    pallas_call x1, Pallas kernels, local(): pl.pallas_call(functools.partial(kernel, (C, D, H, W, segs, n, scale)), o...  20.3 us
    pallas_call x1, Pallas kernels, local(): pl.pallas_call(write_out, out_shape=(pair, pair, pair, share), in_specs=[...  0.82 us

profile of v5, /device:TPU:1, one launch (start us, length us, event | category | flops | bytes accessed | tf_op | source)
XLA Modules:
  0.0 21.8 jit_solution(2701464254202184426)
XLA Ops:
  0.6 20.3 %petra.1 = (bf16[2,256,128]{2,1,0:T(8,128)(2,1)S(1)}, bf16[2,256,128]{2,1,0:T(8,128)(2,1)S(1)}, bf16[2,256,128]{2,1,0:T(8,128)(2,1)S(1)}, f32[2,32,432]{2,1,0:T(8,128)S(1)}) custom-call(bf16[2,256,128]{2,1,0:T(8,128)(2,1)} %bitcast.11, bf16[2,256,128]{2,1,0:T(8,128)(2,1)} %bitcast.12, bf16[2,256,128]{2,1,0:T(8,128)(2,1)} %bitcast.13, ...), custom_call_target="tpu_custom_call" | custom-call | tf_op jit(solution)/shard_map/petra/pallas_call | solution.py:718
  20.9 0.8 %write_out.1 = (bf16[2,256,128]{2,1,0:T(8,128)(2,1)}, bf16[2,256,128]{2,1,0:T(8,128)(2,1)}, bf16[2,256,128]{2,1,0:T(8,128)(2,1)}, f32[2,32,432]{2,1,0:T(8,128)}) custom-call(bf16[2,256,128]{2,1,0:T(8,128)(2,1)S(1)} %get-tuple-element.12.refs_0_, bf16[2,256,128]{2,1,0:T(8,128)(2,1)S(1)} %get-tuple-element.13.refs_1_, ...), custom_call_target="tpu_custom_call" | custom-call | tf_op jit(solution)/shard_map/write_out/pallas_call | solution.py:777

commit v6 on v5

--- a/solution.py
+++ b/solution.py
@@ -29,7 +29,7 @@
 
 def kernel(
     dims, fwd_hbm, bout_hbm, bgrad_hbm, nxt_hbm, loss_hbm, kern_hbm, fout, backs, grads, dw,
-    fwd, bout, bgrad, nxt, loss, kern, kt, w, dt, pad, stage, second, edge, rest, made, nat, acc,
+    fwd, bout, bgrad, nxt, loss, kern, kt, w, pairs, dt, pad, stage, second, edge, rest, made, nat, acc,
     g3, dsum, dpart, dgot, halo_s, halo_r, seg_s, seg_r, back_s, back_r, edge_s, edge_r, pass_s,
     out_s, d_s, d_r, in_s, ready_s,
 ):
@@ -129,11 +129,19 @@
         def tap(t):
             return kt[pl.ds(t, C, stride=27), :]
 
+        def set_weights(m, a, c, block):
+            here = pl.ds(c * C, C)
+            w[m, a, here, :] = block
+            if a < 2:
+                pairs[m, a, here, 0 : 3 * C] = block
+            if a > 0:
+                pairs[m, a - 1, here, 3 * C : 6 * C] = block
+
         for a in range(3):
             for c in range(3):
                 block = jnp.concatenate([tap(9 * a + 3 * b + c) for b in range(3)], axis=0).T
                 for f in range(2):
-                    w[F + f, a, c * C : (c + 1) * C, :] = block[f * C : (f + 1) * C].astype(bf16)
+                    set_weights(F + f, a, c, block[f * C : (f + 1) * C].astype(bf16))
                 for f in range(2):
                     turned = jnp.concatenate(
                         [
@@ -142,7 +150,7 @@
                         ],
                         axis=1,
                     )
-                    w[FT + f, a, c * C : (c + 1) * C, :] = turned.astype(bf16)
+                    set_weights(FT + f, a, c, turned.astype(bf16))
 
     def load_pair(i, slot, ref):
         fetches[i].wait()
@@ -238,9 +246,15 @@
         return jnp.concatenate([pad[t, k, :, lanes(lane(q, b), HW)] for b in range(3)], axis=0)
 
     def taps(t, k, m, p, which):
-        total = None
-        for a in which:
-            part = jnp.dot(w[m, a], tall(t, k, p + a - 1), preferred_element_type=f32)
+        total, which = None, list(which)
+        while which:
+            a = which.pop(0)
+            lhs, rhs = w[m, a], tall(t, k, p + a - 1)
+            if which:
+                which.pop(0)
+                lhs = pairs[m, a]
+                rhs = jnp.concatenate([rhs, tall(t, k, p + a)], axis=0)
+            part = jnp.dot(lhs, rhs, preferred_element_type=f32)
             total = part if total is None else total + part
         return total
 
@@ -349,6 +363,25 @@
             stage[k, pl.ds(r, C, stride=DH), :] = wide
         return wide
 
+    def straight(first, side):
+        return jnp.logical_and(lax.rem(seg, 4) == first, side == 1)
+
+    def far_direct(side, slot, peer):
+        @pl.when(straight(2, side))
+        def _():
+            for k in (O1, G2):
+                edge_copy(made.at[0, k], k, True, prev_seg, 0, side, slot, peer).start()
+
+    def far_relay(k):
+        def act(side, slot, peer):
+            @pl.when(jnp.logical_not(straight(1, side)))
+            def _():
+                edge_copy(second.at[k], k, True, seg, 3, side, slot, peer).start()
+
+        @pl.when(relayed)
+        def _():
+            over(toward, act)
+
     def hand_on(k):
         src = made.at[0, k]
         if k <= X2:
@@ -371,7 +404,7 @@
                 if k == O1:
                     edge_start(src, O1, False, prev_seg, 0)
                     edge_start(made.at[0, G2], G2, False, prev_seg, 0)
-                    pl.when(even)(functools.partial(edge_start, src, O1, True, prev_seg, 0))
+                    over(toward, far_direct)
 
     def hand_on_far():
         @pl.when(odd)
@@ -472,9 +505,6 @@
 
     conv_finish(0, PD, GT, 0, act, functools.partial(halo_start, 0, PE))
     hand_on(E1)
-    conv_local(0, PE, FT, 0)
-    for r in range(DH):
-        widen(0, r, made[0, E1, :, pl.ds(r * W, W)].astype(f32))
     halo_arrived(0, PH)
 
     def act(r, p, h, out):
@@ -491,6 +521,9 @@
 
     conv_finish(0, PX, F, 2, act, functools.partial(halo_start, 0, PY))
     hand_on(Y1)
+    conv_local(0, PE, FT, 0)
+    for r in range(DH):
+        widen(0, r, made[0, E1, :, pl.ds(r * W, W)].astype(f32))
     conv_local(0, PY, G, 2)
     wgrad_inner(0, PU, 0)
 
@@ -554,16 +587,15 @@
         conv_local(1, PY, G, 2)
 
     arrived(G2)
-
-    @pl.when(relayed)
-    def _():
-        edge_start(second.at[G2], G2, True, seg, 3)
+    far_relay(G2)
 
     pl.when(odd)(forward_own)
     for d in range(D):
         pad[1, PD, :, pl.ds(lane(d, 1), HW)] = second[G2, :, pl.ds(d * HW, HW)]
     conv_local(1, PD, GT, 0)
     arrived(O1)
+    far_relay(O1)
+
     for r in range(DH):
         put(1, PH, r, silu(got(O1, r)))
     conv_local(1, PH, G, 1)
@@ -572,16 +604,22 @@
     wgrad_inner(1, PH, 1)
     pl.when(odd)(forward)
 
-    def edges_in(far, side, slot, peer):
-        q = near_q(side) + (2 * side - 1 if far else 0)
-        at = (side if far else 1 - side) * HW
+    def edge_q(far, side):
+        return near_q(side) + (2 * side - 1 if far else 0), (side if far else 1 - side) * HW
+
+    def grad_in(far, side, slot, peer):
+        q, at = edge_q(far, side)
         edge_arrived(G2, far, side, slot, peer)
         pad[1, PD, :, lanes(lane(q, 1), HW)] = edge[G2, slot, :, lanes(at, HW)]
+
+    def act_in(far, side, slot, peer):
+        q, at = edge_q(far, side)
         edge_arrived(O1, far, side, slot, peer)
         for h in range(H):
             put_at(1, PH, q, h, silu(edge[O1, slot, :, lanes(at + h * W, W)].astype(f32)))
 
-    over(sides, functools.partial(edges_in, False))
+    over(sides, functools.partial(grad_in, False))
+    over(sides, functools.partial(act_in, False))
     arrived(G1)
 
     def act(r, p, h, out):
@@ -594,29 +632,39 @@
         put_at(1, PU, p, h, silu(keep(1, R2, r, got(O2, r) - out)))
 
     conv_finish(1, PH, G, 1, act)
+
+    def give_first():
+        give_out(E1)
+        give_out(R2)
+
+    pl.when(even)(give_first)
+    wgrad_outer(1, PH, 1)
+    wgrad_share(1)
+
+    def beyond_act(side, slot, peer):
+        act_in(True, side, slot, peer)
+        edge_arrived(O2, False, side, slot, peer)
+        q = near_q(side)
+        for h, out in rows_of(taps(1, PH, G, q, range(3))):
+            value = (near(O2, side, slot, h) - out).astype(bf16).astype(f32)
+            put_at(1, PU, q, h, silu(value))
+
+    over(sides, beyond_act)
     for r in range(DH):
         widen(0, r, made[1, E1, :, pl.ds(r * W, W)].astype(f32))
-
-    def beyond(side, slot, peer):
-        edges_in(True, side, slot, peer)
+    wgrad_whole(PU, 0)
+    wgrad_share(0)
+
+    def beyond_grad(side, slot, peer):
+        grad_in(True, side, slot, peer)
         edge_arrived(G1, False, side, slot, peer)
-        edge_arrived(O2, False, side, slot, peer)
         q = near_q(side)
-        turned, plain = taps(1, PD, GT, q, range(3)), taps(1, PH, G, q, range(3))
-        for h, out in rows_of(turned):
+        for h, out in rows_of(taps(1, PD, GT, q, range(3))):
             value = near(G1, side, slot, h) + slope(near(O1, side, slot, h)) * out
             put_at(1, PE, q, h, value)
-        for h, out in rows_of(plain):
-            value = (near(O2, side, slot, h) - out).astype(bf16).astype(f32)
-            put_at(1, PU, q, h, silu(value))
-
-    over(sides, beyond)
-    wgrad_whole(PU, 0)
-    wgrad_share(0)
-    wgrad_outer(1, PH, 1)
-    wgrad_share(1)
-    give_out(E1)
-    give_out(R2)
+
+    over(sides, beyond_grad)
+    pl.when(odd)(give_first)
 
 
     for r, out in conv_whole(1, PE, FT):
@@ -628,7 +676,7 @@
     give_out(R1)
 
     def gradients():
-        for j in (0, 1):
+        for j in (1, 0):
             for q in range(1, n):
                 share(j, q).wait_recv()
             for ab in range(9):
@@ -653,6 +701,15 @@
     give_out(Y2)
     pl.when(odd)(gradients)
 
+    def drain_edges(which, first, fewer, more):
+        def act(side, slot, peer):
+            direct = straight(first, side)
+            sem = edge_s.at[which, slot]
+            pl.when(direct)(lambda: drain(sem, planes_of(more)))
+            pl.when(jnp.logical_not(direct))(lambda: drain(sem, planes_of(fewer)))
+
+        over(toward, act)
+
     over(toward, lambda side, slot, peer: drain(halo_s.at[slot], planes_of(7)))
     for q in range(1, n):
         drain(d_s.at[q - 1], dpart.at[:, 0])
@@ -680,7 +737,7 @@
 
         @pl.when(even)
         def _():
-            over(toward, lambda side, slot, peer: drain(edge_s.at[0, slot], planes_of(3)))
+            drain_edges(0, 2, 2, 4)
 
     @pl.when(odd)
     def _():
@@ -689,7 +746,7 @@
 
     @pl.when(relayed)
     def _():
-        over(toward, lambda side, slot, peer: drain(edge_s.at[3, slot], planes_of(3)))
+        drain_edges(3, 1, 4, 2)
 
 
 def write_out(*refs):
@@ -729,6 +786,7 @@
             pltpu.VMEM((2 * C, 27 * C), bf16),
             pltpu.VMEM((27 * C, wide), f32),
             pltpu.VMEM((4, 3, 3 * C, 3 * C), bf16),
+            pltpu.VMEM((4, 2, 3 * C, 6 * C), bf16),
             pltpu.VMEM((2, 27 * cs, wide), f32),
             pltpu.VMEM((2, 6, C, (D + 4) * (H + 2) * W), bf16),
             pltpu.VMEM((8, rows, W), f32),

time: 21.9 us -> 21.1 us (0.963)
  Pallas kernels: 21.1 us -> 20.3 us
    pallas_call x1, Pallas kernels: 20.3 us -> 19.5 us  [local(): pl.pallas_call(functools.partial(kernel, (C, D, H, W, segs, n, scale)), o...]
where the time goes in v6:
time: 21.1 us; the launch traced here: 20.9 us
  Pallas kernels  20.3 us (96%)
  between operations  0.64 us (3%)
    pallas_call x1, Pallas kernels, local(): pl.pallas_call(functools.partial(kernel, (C, D, H, W, segs, n, scale)), o...  19.5 us
    pallas_call x1, Pallas kernels, local(): pl.pallas_call(write_out, out_shape=(pair, pair, pair, share), in_specs=[...  0.82 us

profile of v6, /device:TPU:1, one launch (start us, length us, event | category | flops | bytes accessed | tf_op | source)
XLA Modules:
  0.0 20.9 jit_solution(18114268852672861886)
XLA Ops:
  0.6 19.5 %petra.1 = (bf16[2,256,128]{2,1,0:T(8,128)(2,1)S(1)}, bf16[2,256,128]{2,1,0:T(8,128)(2,1)S(1)}, bf16[2,256,128]{2,1,0:T(8,128)(2,1)S(1)}, f32[2,32,432]{2,1,0:T(8,128)S(1)}) custom-call(bf16[2,256,128]{2,1,0:T(8,128)(2,1)} %bitcast.11, bf16[2,256,128]{2,1,0:T(8,128)(2,1)} %bitcast.12, bf16[2,256,128]{2,1,0:T(8,128)(2,1)} %bitcast.13, ...), custom_call_target="tpu_custom_call" | custom-call | tf_op jit(solution)/shard_map/petra/pallas_call | solution.py:775
  20.1 0.8 %write_out.1 = (bf16[2,256,128]{2,1,0:T(8,128)(2,1)}, bf16[2,256,128]{2,1,0:T(8,128)(2,1)}, bf16[2,256,128]{2,1,0:T(8,128)(2,1)}, f32[2,32,432]{2,1,0:T(8,128)}) custom-call(bf16[2,256,128]{2,1,0:T(8,128)(2,1)S(1)} %get-tuple-element.12.refs_0_, bf16[2,256,128]{2,1,0:T(8,128)(2,1)S(1)} %get-tuple-element.13.refs_1_, ...), custom_call_target="tpu_custom_call" | custom-call | tf_op jit(solution)/shard_map/write_out/pallas_call | solution.py:835

commit v7 on v6

--- a/solution.py
+++ b/solution.py
@@ -364,7 +364,7 @@
         return wide
 
     def straight(first, side):
-        return jnp.logical_and(lax.rem(seg, 4) == first, side == 1)
+        return lax.rem(seg, 4) == first
 
     def far_direct(side, slot, peer):
         @pl.when(straight(2, side))
@@ -618,20 +618,20 @@
         for h in range(H):
             put_at(1, PH, q, h, silu(edge[O1, slot, :, lanes(at + h * W, W)].astype(f32)))
 
+    over(sides, functools.partial(act_in, False))
+    arrived(O2)
+
+    def act(r, p, h, out):
+        put_at(1, PU, p, h, silu(keep(1, R2, r, got(O2, r) - out)))
+
+    conv_finish(1, PH, G, 1, act)
     over(sides, functools.partial(grad_in, False))
-    over(sides, functools.partial(act_in, False))
     arrived(G1)
 
     def act(r, p, h, out):
         put_at(1, PE, p, h, keep(1, E1, r, got(G1, r) + slope(got(O1, r)) * out))
 
     conv_finish(1, PD, GT, 0, act)
-    arrived(O2)
-
-    def act(r, p, h, out):
-        put_at(1, PU, p, h, silu(keep(1, R2, r, got(O2, r) - out)))
-
-    conv_finish(1, PH, G, 1, act)
 
     def give_first():
         give_out(E1)

time: 21.1 us -> 20.9 us (level)
    pallas_call x1, Pallas kernels: 19.5 us -> 19.2 us  [local(): pl.pallas_call(functools.partial(kernel, (C, D, H, W, segs, n, scale)), o...]
where the time goes in v7:
time: 20.9 us; the launch traced here: 20.7 us
  Pallas kernels  20.1 us (96%)
  between operations  0.64 us (3%)
    pallas_call x1, Pallas kernels, local(): pl.pallas_call(functools.partial(kernel, (C, D, H, W, segs, n, scale)), o...  19.2 us
    pallas_call x1, Pallas kernels, local(): pl.pallas_call(write_out, out_shape=(pair, pair, pair, share), in_specs=[...  0.82 us

profile of v7, /device:TPU:1, one launch (start us, length us, event | category | flops | bytes accessed | tf_op | source)
XLA Modules:
  0.0 20.7 jit_solution(4680879504578233464)
XLA Ops:
  0.6 19.2 %petra.1 = (bf16[2,256,128]{2,1,0:T(8,128)(2,1)S(1)}, bf16[2,256,128]{2,1,0:T(8,128)(2,1)S(1)}, bf16[2,256,128]{2,1,0:T(8,128)(2,1)S(1)}, f32[2,32,432]{2,1,0:T(8,128)S(1)}) custom-call(bf16[2,256,128]{2,1,0:T(8,128)(2,1)} %bitcast.11, bf16[2,256,128]{2,1,0:T(8,128)(2,1)} %bitcast.12, bf16[2,256,128]{2,1,0:T(8,128)(2,1)} %bitcast.13, ...), custom_call_target="tpu_custom_call" | custom-call | tf_op jit(solution)/shard_map/petra/pallas_call | solution.py:775
  19.9 0.8 %write_out.1 = (bf16[2,256,128]{2,1,0:T(8,128)(2,1)}, bf16[2,256,128]{2,1,0:T(8,128)(2,1)}, bf16[2,256,128]{2,1,0:T(8,128)(2,1)}, f32[2,32,432]{2,1,0:T(8,128)}) custom-call(bf16[2,256,128]{2,1,0:T(8,128)(2,1)S(1)} %get-tuple-element.12.refs_0_, bf16[2,256,128]{2,1,0:T(8,128)(2,1)S(1)} %get-tuple-element.13.refs_1_, ...), custom_call_target="tpu_custom_call" | custom-call | tf_op jit(solution)/shard_map/write_out/pallas_call | solution.py:835

commit v8 on v7

--- a/solution.py
+++ b/solution.py
@@ -601,7 +601,6 @@
     conv_local(1, PH, G, 1)
     for r in range(DH):
         widen(1, r, got(G2, r))
-    wgrad_inner(1, PH, 1)
     pl.when(odd)(forward)
 
     def edge_q(far, side):
@@ -638,7 +637,7 @@
         give_out(R2)
 
     pl.when(even)(give_first)
-    wgrad_outer(1, PH, 1)
+    wgrad_whole(PH, 1)
     wgrad_share(1)
 
     def beyond_act(side, slot, peer):

time: 20.9 us -> 20.9 us (level)
  no operation moved by 1% of the time
where the time goes in v8:
time: 20.9 us; the launch traced here: 20.7 us
  Pallas kernels  20.1 us (96%)
  between operations  0.64 us (3%)
    pallas_call x1, Pallas kernels, local(): pl.pallas_call(functools.partial(kernel, (C, D, H, W, segs, n, scale)), o...  19.2 us
    pallas_call x1, Pallas kernels, local(): pl.pallas_call(write_out, out_shape=(pair, pair, pair, share), in_specs=[...  0.82 us

profile of v8, /device:TPU:1, one launch (start us, length us, event | category | flops | bytes accessed | tf_op | source)
XLA Modules:
  0.0 20.7 jit_solution(16316456728612841879)
XLA Ops:
  0.6 19.2 %petra.1 = (bf16[2,256,128]{2,1,0:T(8,128)(2,1)S(1)}, bf16[2,256,128]{2,1,0:T(8,128)(2,1)S(1)}, bf16[2,256,128]{2,1,0:T(8,128)(2,1)S(1)}, f32[2,32,432]{2,1,0:T(8,128)S(1)}) custom-call(bf16[2,256,128]{2,1,0:T(8,128)(2,1)} %bitcast.11, bf16[2,256,128]{2,1,0:T(8,128)(2,1)} %bitcast.12, bf16[2,256,128]{2,1,0:T(8,128)(2,1)} %bitcast.13, ...), custom_call_target="tpu_custom_call" | custom-call | tf_op jit(solution)/shard_map/petra/pallas_call | solution.py:774
  19.9 0.8 %write_out.1 = (bf16[2,256,128]{2,1,0:T(8,128)(2,1)}, bf16[2,256,128]{2,1,0:T(8,128)(2,1)}, bf16[2,256,128]{2,1,0:T(8,128)(2,1)}, f32[2,32,432]{2,1,0:T(8,128)}) custom-call(bf16[2,256,128]{2,1,0:T(8,128)(2,1)S(1)} %get-tuple-element.12.refs_0_, bf16[2,256,128]{2,1,0:T(8,128)(2,1)S(1)} %get-tuple-element.13.refs_1_, ...), custom_call_target="tpu_custom_call" | custom-call | tf_op jit(solution)/shard_map/write_out/pallas_call | solution.py:834

commit v9 on v8

--- a/solution.py
+++ b/solution.py
@@ -583,6 +583,8 @@
             put_at(1, PY, p, h, silu(keep(1, Y1, r, got(X1, r) + out)))
 
         conv_finish(1, PX, F, 2, act, functools.partial(halo_start, 1, PY))
+
+    def forward_rest():
         give_out(Y1)
         conv_local(1, PY, G, 2)
 
@@ -663,7 +665,11 @@
             put_at(1, PE, q, h, value)
 
     over(sides, beyond_grad)
-    pl.when(odd)(give_first)
+
+    @pl.when(odd)
+    def _():
+        give_first()
+        forward_rest()
 
 
     for r, out in conv_whole(1, PE, FT):
@@ -693,6 +699,7 @@
     def _():
         forward_own()
         forward()
+        forward_rest()
         gradients()
 
     halo_arrived(1, PY)

time: 20.9 us -> 20.9 us (level)
  no operation moved by 1% of the time
where the time goes in v9:
time: 20.9 us; the launch traced here: 20.7 us
  Pallas kernels  20.1 us (96%)
  between operations  0.64 us (3%)
    pallas_call x1, Pallas kernels, local(): pl.pallas_call(functools.partial(kernel, (C, D, H, W, segs, n, scale)), o...  19.2 us
    pallas_call x1, Pallas kernels, local(): pl.pallas_call(write_out, out_shape=(pair, pair, pair, share), in_specs=[...  0.82 us

profile of v9, /device:TPU:1, one launch (start us, length us, event | category | flops | bytes accessed | tf_op | source)
XLA Modules:
  0.0 20.7 jit_solution(9573424723596567028)
XLA Ops:
  0.6 19.2 %petra.1 = (bf16[2,256,128]{2,1,0:T(8,128)(2,1)S(1)}, bf16[2,256,128]{2,1,0:T(8,128)(2,1)S(1)}, bf16[2,256,128]{2,1,0:T(8,128)(2,1)S(1)}, f32[2,32,432]{2,1,0:T(8,128)S(1)}) custom-call(bf16[2,256,128]{2,1,0:T(8,128)(2,1)} %bitcast.11, bf16[2,256,128]{2,1,0:T(8,128)(2,1)} %bitcast.12, bf16[2,256,128]{2,1,0:T(8,128)(2,1)} %bitcast.13, ...), custom_call_target="tpu_custom_call" | custom-call | tf_op jit(solution)/shard_map/petra/pallas_call | solution.py:781
  19.9 0.8 %write_out.1 = (bf16[2,256,128]{2,1,0:T(8,128)(2,1)}, bf16[2,256,128]{2,1,0:T(8,128)(2,1)}, bf16[2,256,128]{2,1,0:T(8,128)(2,1)}, f32[2,32,432]{2,1,0:T(8,128)}) custom-call(bf16[2,256,128]{2,1,0:T(8,128)(2,1)S(1)} %get-tuple-element.12.refs_0_, bf16[2,256,128]{2,1,0:T(8,128)(2,1)S(1)} %get-tuple-element.13.refs_1_, ...), custom_call_target="tpu_custom_call" | custom-call | tf_op jit(solution)/shard_map/write_out/pallas_call | solution.py:841

commit v10 on v9

--- a/solution.py
+++ b/solution.py
@@ -583,9 +583,6 @@
             put_at(1, PY, p, h, silu(keep(1, Y1, r, got(X1, r) + out)))
 
         conv_finish(1, PX, F, 2, act, functools.partial(halo_start, 1, PY))
-
-    def forward_rest():
-        give_out(Y1)
         conv_local(1, PY, G, 2)
 
     arrived(G2)
@@ -669,7 +666,7 @@
     @pl.when(odd)
     def _():
         give_first()
-        forward_rest()
+        give_out(Y1)
 
 
     for r, out in conv_whole(1, PE, FT):
@@ -699,7 +696,7 @@
     def _():
         forward_own()
         forward()
-        forward_rest()
+        give_out(Y1)
         gradients()
 
     halo_arrived(1, PY)

time: 20.9 us -> 20.9 us (level)
  no operation moved by 1% of the time
where the time goes in v10:
time: 20.9 us; the launch traced here: 20.7 us
  Pallas kernels  20.1 us (96%)
  between operations  0.64 us (3%)
    pallas_call x1, Pallas kernels, local(): pl.pallas_call(functools.partial(kernel, (C, D, H, W, segs, n, scale)), o...  19.2 us
    pallas_call x1, Pallas kernels, local(): pl.pallas_call(write_out, out_shape=(pair, pair, pair, share), in_specs=[...  0.82 us

profile of v10, /device:TPU:1, one launch (start us, length us, event | category | flops | bytes accessed | tf_op | source)
XLA Modules:
  0.0 20.7 jit_solution(158960854044511195)
XLA Ops:
  0.6 19.2 %petra.1 = (bf16[2,256,128]{2,1,0:T(8,128)(2,1)S(1)}, bf16[2,256,128]{2,1,0:T(8,128)(2,1)S(1)}, bf16[2,256,128]{2,1,0:T(8,128)(2,1)S(1)}, f32[2,32,432]{2,1,0:T(8,128)S(1)}) custom-call(bf16[2,256,128]{2,1,0:T(8,128)(2,1)} %bitcast.11, bf16[2,256,128]{2,1,0:T(8,128)(2,1)} %bitcast.12, bf16[2,256,128]{2,1,0:T(8,128)(2,1)} %bitcast.13, ...), custom_call_target="tpu_custom_call" | custom-call | tf_op jit(solution)/shard_map/petra/pallas_call | solution.py:778
  19.9 0.8 %write_out.1 = (bf16[2,256,128]{2,1,0:T(8,128)(2,1)}, bf16[2,256,128]{2,1,0:T(8,128)(2,1)}, bf16[2,256,128]{2,1,0:T(8,128)(2,1)}, f32[2,32,432]{2,1,0:T(8,128)}) custom-call(bf16[2,256,128]{2,1,0:T(8,128)(2,1)S(1)} %get-tuple-element.12.refs_0_, bf16[2,256,128]{2,1,0:T(8,128)(2,1)S(1)} %get-tuple-element.13.refs_1_, ...), custom_call_target="tpu_custom_call" | custom-call | tf_op jit(solution)/shard_map/write_out/pallas_call | solution.py:838
